TPU v7x, 128 devices: a whole 4x4x4 slice. The times are simulated.
128 devices in a mesh: lat: 16 (over x, z), dep: 8 (over y, core).
Axes of the slice: x: 4, y: 4, z: 4, core: 2. Of those that a mesh axis runs over, the one named last changes fastest.
Arguments:
- state: float32 [64, 64, 128], P('lat', 'dep'), may hold values from 0.2 to 1
- kappa: float32 [64, 64, 128], P('lat', 'dep'), may hold values from 0.3 to 3
- rate: float32 [64, 64], P('lat', 'dep'), may hold values from 1 to 4
- grads: float32 [3, 64, 64], replicated, may hold values from -0.75 to 0.75
- lift: float32 [4, 32, 128], replicated, may hold values from -0.375 to 0.375
- rhs: float32 [64, 64, 32, 128], P('lat', 'dep'), may hold values from -18 to 18
Outputs:
- update: float32 [64, 64, 32, 128], P('lat', 'dep')
All inputs are finite; a program needn't handle non-finite values.
Results may differ from a plain program's by a relative error of at most 0.0003.
Values sent between devices are 32-bit elements; how exact they have to be, the bound alone decides.
A program may use at most 128 MiB of HBM per device.

v0:
```python
import jax
import jax.numpy as jnp
from jax import lax
from jax.sharding import PartitionSpec as P

KRY = 8


highest = lax.Precision.HIGHEST
mass_shift = 0.25


def with_halo(cells, sides, width, closed):
    for axis, dim in sides:
        count = lax.axis_size(axis)
        ends = count if closed else count - 1
        head = lax.slice_in_dim(cells, 0, width, axis=dim)
        tail = lax.slice_in_dim(cells, cells.shape[dim] - width, cells.shape[dim], axis=dim)
        cells = jnp.concatenate(
            [
                lax.ppermute(tail, axis, [(i, (i + 1) % count) for i in range(ends)]),
                cells,
                lax.ppermute(head, axis, [((i + 1) % count, i) for i in range(ends)]),
            ],
            axis=dim,
        )
    return cells


def from_behind(value, axis, steps):
    count = lax.axis_size(axis)
    pairs = [(source, (source + steps) % count) for source in range(count)]
    return lax.ppermute(value, axis, pairs)


def passed_along(array, axis, by):
    peers = lax.axis_size(axis)
    pairs = [(i, i + by) for i in range(peers) if 0 <= i + by < peers]
    return lax.ppermute(array, axis, pairs)


def face_table():
    unknown = jnp.arange(128, dtype=jnp.int32)[:, None]
    column = jnp.arange(128, dtype=jnp.int32)[None, :]
    face_id = column // 32
    species = column // 16 % 2
    along_one = column % 16 // 4
    along_two = column % 4
    edge_pos = 3 * (face_id % 2)
    is_lateral = face_id < 2
    node_x = jnp.where(is_lateral, edge_pos, along_one)
    node_y = jnp.where(is_lateral, along_one, along_two)
    node_z = jnp.where(is_lateral, along_two, edge_pos)
    target = species * 64 + node_x * 16 + node_y * 4 + node_z
    return (unknown == target).astype(jnp.float32)


def pairing_table():
    unknown = jnp.arange(128, dtype=jnp.int32)
    return (unknown[:, None] % 64 == unknown[None, :] % 64).astype(jnp.float32)


def element_tiles(kappa_rows, state_rows, rate_rows, grads, select):
    row_count = kappa_rows.shape[0]
    split_kappa = kappa_rows.reshape(row_count, 2, 64)
    stiffness = jnp.einsum("dqi,nsq,dqj->nsij", grads, split_kappa, grads, precision=highest)
    zero_block = jnp.zeros((row_count, 64, 64), jnp.float32)
    top_half = jnp.concatenate([stiffness[:, 0], zero_block], axis=2)
    bottom_half = jnp.concatenate([zero_block, stiffness[:, 1]], axis=2)
    face_kappa = jnp.dot(kappa_rows, select, precision=highest)
    penalty = jnp.dot(face_kappa, select.T, precision=highest)
    partner = jnp.concatenate([state_rows[:, 64:], state_rows[:, :64]], axis=1)
    identity = jnp.eye(128, dtype=jnp.float32)
    diag_tiles = jnp.concatenate([top_half, bottom_half], axis=1)
    diag_tiles = diag_tiles + identity[None] * (mass_shift + penalty)[:, None, :]
    diag_tiles = diag_tiles + pairing_table()[None] * (rate_rows[:, None] * partner)[:, None, :]
    return (diag_tiles, face_kappa)


def apply_operator(vectors, diag_tiles, couple, select):
    lat_rows = vectors.shape[0]
    dep_rows = vectors.shape[1]
    columns = vectors.shape[2]
    traces = jnp.einsum("aevu,uk->aevk", vectors, select, precision=highest)
    lat_rims = jnp.stack([traces[0, :, :, 0:32], traces[-1, :, :, 32:64]]).reshape(
        2, dep_rows, columns * 32
    )
    lat_wide = with_halo(lat_rims, (("lat", 0),), 1, True)
    prev_lat = lat_wide[0].reshape(dep_rows, columns, 32)
    next_lat = lat_wide[3].reshape(dep_rows, columns, 32)
    dep_rims = jnp.stack([traces[:, 0, :, 64:96], traces[:, -1, :, 96:128]]).reshape(
        2, lat_rows, columns * 32
    )
    dep_wide = with_halo(dep_rims, (("dep", 0),), 1, False)
    prev_dep = dep_wide[0].reshape(lat_rows, columns, 32)
    next_dep = dep_wide[3].reshape(lat_rows, columns, 32)
    from_left = jnp.concatenate([prev_lat[None], traces[:-1, :, :, 32:64]], axis=0)
    from_right = jnp.concatenate([traces[1:, :, :, 0:32], next_lat[None]], axis=0)
    from_below = jnp.concatenate([prev_dep[:, None], traces[:, :-1, :, 96:128]], axis=1)
    from_above = jnp.concatenate([traces[:, 1:, :, 64:96], next_dep[:, None]], axis=1)
    near_traces = jnp.concatenate([from_left, from_right, from_below, from_above], axis=-1)
    own_part = jnp.einsum("aeij,aevj->aevi", diag_tiles, vectors, precision=highest)
    coupled = jnp.einsum("aeki,aevk->aevi", couple, near_traces, precision=highest)
    return own_part - coupled


def inner_local(left_block, right_block):
    return jnp.einsum("aevu,aewu->vw", left_block, right_block, precision=highest)


def combine_columns(vectors, matrix):
    return jnp.einsum("aevu,vw->aewu", vectors, matrix, precision=highest)


def factor(gram_matrix):
    lower_factor = jnp.linalg.cholesky(gram_matrix)
    identity = jnp.eye(gram_matrix.shape[0], dtype=gram_matrix.dtype)
    inverse = jax.scipy.linalg.solve_triangular(lower_factor, identity, lower=True)
    return (lower_factor.T, inverse.T)


def per_device(state, kappa, rate, grads, lift, rhs):
    select = face_table()

    def one_row(row_data):
        return element_tiles(row_data[0], row_data[1], row_data[2], grads, select)

    diag_tiles, face_kappa = lax.map(one_row, (kappa, state, rate))
    lat_end = face_kappa[-1, :, 32:64]
    dep_end = face_kappa[:, -1, 96:128]
    own_right = lift[1] * face_kappa[:, :, 32:64, None]
    own_top = lift[3] * face_kappa[:, :, 96:128, None]
    sent_lat = from_behind(lift[0][None] * lat_end[:, :, None], "lat", 1)
    sent_dep = passed_along(lift[2][None] * dep_end[:, :, None], "dep", 1)
    left_tiles = jnp.concatenate(
        [sent_lat[None], lift[0] * face_kappa[:-1, :, 32:64, None]], axis=0
    )
    below_tiles = jnp.concatenate(
        [sent_dep[:, None], lift[2] * face_kappa[:, :-1, 96:128, None]], axis=1
    )
    couple = jnp.concatenate([left_tiles, own_right, below_tiles, own_top], axis=2)
    columns = rhs.shape[2]
    start_factor, inverse = factor(lax.psum(inner_local(rhs, rhs), ("lat", "dep")))
    basis_list = [combine_columns(rhs, inverse)]
    coef_table = []
    for step_index in range(KRY):
        image_block = apply_operator(basis_list[step_index], diag_tiles, couple, select)
        local_prods = jnp.stack(
            [inner_local(basis_list[prior], image_block) for prior in range(step_index + 1)]
        )
        coef_stack = lax.psum(local_prods, ("lat", "dep"))
        for prior in range(step_index + 1):
            image_block = image_block - combine_columns(basis_list[prior], coef_stack[prior])
        gram_matrix = lax.psum(inner_local(image_block, image_block), ("lat", "dep"))
        upper_factor, inverse = factor(gram_matrix)
        column_coefs = [coef_stack[prior] for prior in range(step_index + 1)]
        column_coefs.append(upper_factor)
        coef_table.append(column_coefs)
        basis_list.append(combine_columns(image_block, inverse))
    zero_small = jnp.zeros((columns, columns), jnp.float32)
    block_rows = []
    for row_index in range(KRY + 1):
        row_blocks = []
        for col_index in range(KRY):
            if row_index <= col_index + 1:
                row_blocks.append(coef_table[col_index][row_index])
            else:
                row_blocks.append(zero_small)
        block_rows.append(jnp.concatenate(row_blocks, axis=1))
    hessenberg = jnp.concatenate(block_rows, axis=0)
    gram_small = jnp.dot(hessenberg.T, hessenberg, precision=highest)
    right_side = jnp.dot(hessenberg[:columns].T, start_factor, precision=highest)
    coeffs = jax.scipy.linalg.cho_solve((jnp.linalg.cholesky(gram_small), True), right_side)
    update = combine_columns(basis_list[0], coeffs[:columns])
    for step_index in range(1, KRY):
        update = update + combine_columns(
            basis_list[step_index], coeffs[step_index * columns : (step_index + 1) * columns]
        )
    return update


def solution(mesh):
    in_specs = (
        P("lat", "dep", None),
        P("lat", "dep", None),
        P("lat", "dep"),
        P(),
        P(),
        P("lat", "dep", None, None),
    )
    out_specs = P("lat", "dep", None, None)
    return jax.shard_map(
        per_device, mesh=mesh, in_specs=in_specs, out_specs=out_specs, check_vma=False
    )
```

profile of v0, /device:TPU:1, one launch (start us, length us, event | category | flops | bytes accessed | tf_op | source)
XLA Modules:
  0.0 1614.5 jit_solution(5282608771596217027)
XLA Ops:
  1.6 68.8 %psum.119 = f32[32,32]{0,1:T(8,128)S(1)} all-reduce(f32[32,32]{0,1:T(8,128)S(1)} %convolution_bitcast_fusion.97), channel_id=1, replica_groups=mesh['lat'=16,'dep'=8] {'lat','dep'}, use_global_device_ids=true, to_apply=%region_0.1 | all-reduce | flops 1024 | bytes 8192 | tf_op jit(solution)/shard_map/psum | solution.py:143
  79.8 4.8 collective-permute-start.1
  91.2 50.8 %while.18 = (s32[]{:T(128)}, f32[4,8,128,128]{3,2,1,0:T(8,128)S(1)}, f32[4,8,128]{2,1,0:T(8,128)S(1)}, f32[3,64,64]{2,0,1:T(4,128)S(1)}, f32[4,8,128]{2,1,0:T(8,...) while((s32[]{:T(128)}, ...), condition=%wide.region_4.7_spmd.clone.clone, body=%wide.region_3.6_spmd.clone.clone.sunk | while | flops 63704832 | bytes 7220429 | solution.py:128
  172.6 65.2 %psum.120 = f32[32,32]{0,1:T(8,128)S(1)} all-reduce(f32[32,32]{0,1:T(8,128)} %convolution_bitcast_fusion.95), channel_id=1, replica_groups=mesh['lat'=16,'dep'=8] {'lat','dep'}, use_global_device_ids=true, to_apply=%region_5.8 | all-reduce | flops 1024 | bytes 8192 | tf_op jit(solution)/shard_map/psum | solution.py:151
  240.1 64.2 %psum.121 = f32[32,32]{0,1:T(8,128)S(1)} all-reduce(f32[32,32]{0,1:T(8,128)S(1)} %convolution_bitcast_fusion.94), channel_id=1, replica_groups=mesh['lat'=16,'dep'=8] {'lat','dep'}, use_global_device_ids=true, to_apply=%region_6.9 | all-reduce | flops 1024 | bytes 8192 | tf_op jit(solution)/shard_map/psum | solution.py:154
  322.7 4.8 collective-permute-start.7
  338.7 4.3 convolution_subtract_fusion.6
  344.4 62.0 %psum.122 = f32[2,32,32]{1,2,0:T(8,128)S(1)} all-reduce(f32[2,32,32]{1,2,0:T(8,128)S(1)} %pad_maximum_fusion.5), channel_id=1, replica_groups=mesh['lat'=16,'dep'=8] {'lat','dep'}, use_global_device_ids=true, to_apply=%region_7.10 | all-reduce | flops 2048 | bytes 16384 | tf_op jit(solution)/shard_map/psum | solution.py:151
  410.1 63.5 %psum.123 = f32[32,32]{0,1:T(8,128)S(1)} all-reduce(f32[32,32]{0,1:T(8,128)S(1)} %convolution_bitcast_fusion.90), channel_id=1, replica_groups=mesh['lat'=16,'dep'=8] {'lat','dep'}, use_global_device_ids=true, to_apply=%region_8.11 | all-reduce | flops 1024 | bytes 8192 | tf_op jit(solution)/shard_map/psum | solution.py:154
  490.8 4.8 collective-permute-start.11
  513.9 62.9 %psum.124 = f32[3,32,32]{1,2,0:T(8,128)S(1)} all-reduce(f32[3,32,32]{1,2,0:T(8,128)S(1)} %pad_maximum_fusion.4), channel_id=1, replica_groups=mesh['lat'=16,'dep'=8] {'lat','dep'}, use_global_device_ids=true, to_apply=%region_9.12 | all-reduce | flops 3072 | bytes 24576 | tf_op jit(solution)/shard_map/psum | solution.py:151
  581.1 64.3 %psum.125 = f32[32,32]{0,1:T(8,128)S(1)} all-reduce(f32[32,32]{0,1:T(8,128)S(1)} %convolution_bitcast_fusion.85), channel_id=1, replica_groups=mesh['lat'=16,'dep'=8] {'lat','dep'}, use_global_device_ids=true, to_apply=%region_10.13 | all-reduce | flops 1024 | bytes 8192 | tf_op jit(solution)/shard_map/psum | solution.py:154
  662.6 4.8 collective-permute-start.15
  685.9 63.0 %psum.126 = f32[4,32,32]{1,2,0:T(8,128)S(1)} all-reduce(f32[4,32,32]{1,2,0:T(8,128)S(1)} %pad_maximum_fusion.3), channel_id=1, replica_groups=mesh['lat'=16,'dep'=8] {'lat','dep'}, use_global_device_ids=true, to_apply=%region_11.14 | all-reduce | flops 4096 | bytes 32768 | tf_op jit(solution)/shard_map/psum | solution.py:151
  753.7 63.5 %psum.127 = f32[32,32]{0,1:T(8,128)S(1)} all-reduce(f32[32,32]{0,1:T(8,128)S(1)} %convolution_bitcast_fusion.79), channel_id=1, replica_groups=mesh['lat'=16,'dep'=8] {'lat','dep'}, use_global_device_ids=true, to_apply=%region_12.15 | all-reduce | flops 1024 | bytes 8192 | tf_op jit(solution)/shard_map/psum | solution.py:154
  836.5 4.8 collective-permute-start.19
  860.7 62.7 %psum.128 = f32[5,32,32]{1,2,0:T(8,128)S(1)} all-reduce(f32[5,32,32]{1,2,0:T(8,128)S(1)} %fusion.76), channel_id=1, replica_groups=mesh['lat'=16,'dep'=8] {'lat','dep'}, use_global_device_ids=true, to_apply=%region_13.16 | all-reduce | flops 5120 | bytes 40960 | tf_op jit(solution)/shard_map/psum | solution.py:151
  928.8 64.2 %psum.129 = f32[32,32]{0,1:T(8,128)S(1)} all-reduce(f32[32,32]{0,1:T(8,128)S(1)} %convolution_bitcast_fusion.72), channel_id=1, replica_groups=mesh['lat'=16,'dep'=8] {'lat','dep'}, use_global_device_ids=true, to_apply=%region_14.17 | all-reduce | flops 1024 | bytes 8192 | tf_op jit(solution)/shard_map/psum | solution.py:154
  1011.7 4.8 collective-permute-start.23
  1036.6 63.3 %psum.130 = f32[6,32,32]{1,2,0:T(8,128)S(1)} all-reduce(f32[6,32,32]{1,2,0:T(8,128)S(1)} %fusion.70), channel_id=1, replica_groups=mesh['lat'=16,'dep'=8] {'lat','dep'}, use_global_device_ids=true, to_apply=%region_15.18 | all-reduce | flops 6144 | bytes 49152 | tf_op jit(solution)/shard_map/psum | solution.py:151
  1106.0 63.8 %psum.131 = f32[32,32]{0,1:T(8,128)S(1)} all-reduce(f32[32,32]{0,1:T(8,128)S(1)} %convolution_bitcast_fusion.64), channel_id=1, replica_groups=mesh['lat'=16,'dep'=8] {'lat','dep'}, use_global_device_ids=true, to_apply=%region_16.19 | all-reduce | flops 1024 | bytes 8192 | tf_op jit(solution)/shard_map/psum | solution.py:154
  1189.3 4.8 collective-permute-start.27
  1214.6 63.2 %psum.132 = f32[7,32,32]{1,2,0:T(8,128)S(1)} all-reduce(f32[7,32,32]{1,2,0:T(8,128)S(1)} %fusion.63), channel_id=1, replica_groups=mesh['lat'=16,'dep'=8] {'lat','dep'}, use_global_device_ids=true, to_apply=%region_17.20 | all-reduce | flops 7168 | bytes 57344 | tf_op jit(solution)/shard_map/psum | solution.py:151
  1284.5 64.2 %psum.133 = f32[32,32]{0,1:T(8,128)S(1)} all-reduce(f32[32,32]{0,1:T(8,128)S(1)} %convolution_bitcast_fusion.55), channel_id=1, replica_groups=mesh['lat'=16,'dep'=8] {'lat','dep'}, use_global_device_ids=true, to_apply=%region_18.21 | all-reduce | flops 1024 | bytes 8192 | tf_op jit(solution)/shard_map/psum | solution.py:154
  1367.0 4.8 collective-permute-start.31
  1390.9 63.0 %psum.134 = f32[8,32,32]{1,2,0:T(8,128)S(1)} all-reduce(f32[8,32,32]{1,2,0:T(8,128)S(1)} %fusion.55), channel_id=1, replica_groups=mesh['lat'=16,'dep'=8] {'lat','dep'}, use_global_device_ids=true, to_apply=%region_19.22 | all-reduce | flops 8192 | bytes 65536 | tf_op jit(solution)/shard_map/psum | solution.py:151
  1459.3 63.7 %psum.135 = f32[32,32]{0,1:T(8,128)S(1)} all-reduce(f32[32,32]{0,1:T(8,128)S(1)} %convolution_bitcast_fusion.45), channel_id=1, replica_groups=mesh['lat'=16,'dep'=8] {'lat','dep'}, use_global_device_ids=true, to_apply=%region_20.23 | all-reduce | flops 1024 | bytes 8192 | tf_op jit(solution)/shard_map/psum | solution.py:154
  1536.6 11.7 cholesky.77
  1551.2 9.8 custom-call.23
  1563.2 11.7 cholesky.132
  1579.7 5.1 while.17
  1584.8 20.8 %custom-call.24 = f32[2,128,128]{1,2,0:T(8,128)S(1)} custom-call(f32[2,128,128]{2,1,0:T(8,128)} %get-tuple-element.122), custom_call_target="InvertDiagBlocksLowerTriangular" | custom-call | tf_op jit(solution)/shard_map/jit(_cho_solve)/triangular_solve | solution.py:173
  (677 shorter events, 427.5 us)
Async XLA Ops:
  79.1 84.4 %collective-permute-start = (f32[1,8,1024]{2,1,0:T(8,128)}, f32[1,8,1024]{2,1,0:T(8,128)}, u32[]{:S(2)}, u32[]{:S(2)}) collective-permute-start(f32[1,8,1024]{2,1,0:T(8,128)} %slice.619), channel_id=1, source_target_pairs={{0,8},{8,16},{16,24},{24,32},{32,40},{40,48},{48,56},{56,64},{64,7... | collective-permute-start | bytes 98312 | tf_op jit(solution)/shard_map/ppermute | solution.py:21
  79.8 85.2 %collective-permute-start.1 = (f32[1,8,1024]{2,1,0:T(8,128)}, f32[1,8,1024]{2,1,0:T(8,128)}, u32[]{:S(2)}, u32[]{:S(2)}) collective-permute-start(f32[1,8,1024]{2,1,0:T(8,128)} %slice.623), channel_id=1, source_target_pairs={{8,0},{16,8},{24,16},{32,24},{40,32},{48,40},{56,48},{64,56},{72,6... | collective-permute-start | bytes 98312 | tf_op jit(solution)/shard_map/ppermute | solution.py:23
  85.4 70.7 %collective-permute-start.2 = (f32[1,4,1024]{2,1,0:T(4,128)}, f32[1,4,1024]{2,1,0:T(4,128)S(1)}, u32[]{:S(2)}, u32[]{:S(2)}) collective-permute-start(f32[1,4,1024]{2,1,0:T(4,128)} %slice.625), channel_id=1, source_target_pairs={{0,1},{1,2},{2,3},{3,4},{4,5},{5,6},{6,7},{8,9},{9,10},{10,11},{11... | collective-permute-start | bytes 49160 | tf_op jit(solution)/shard_map/ppermute | solution.py:21
  89.1 73.0 %collective-permute-start.3 = (f32[1,4,1024]{2,1,0:T(4,128)}, f32[1,4,1024]{2,1,0:T(4,128)}, u32[]{:S(2)}, u32[]{:S(2)}) collective-permute-start(f32[1,4,1024]{2,1,0:T(4,128)} %slice.629), channel_id=1, source_target_pairs={{1,0},{2,1},{3,2},{4,3},{5,4},{6,5},{7,6},{9,8},{10,9},{11,10},{12... | collective-permute-start | bytes 49160 | tf_op jit(solution)/shard_map/ppermute | solution.py:23
  142.8 23.7 %collective-permute-start.4 = (f32[8,32,128]{2,1,0:T(8,128)}, f32[8,32,128]{2,1,0:T(8,128)}, u32[]{:S(2)}, u32[]{:S(2)}) collective-permute-start(f32[8,32,128]{2,1,0:T(8,128)} %broadcast_multiply_fusion.4), channel_id=1, source_target_pairs={{0,8},{8,16},{16,24},{24,32},{32,40},{40,48},{48,56},{56,64},{64,7... | collective-permute-start | bytes 393224 | tf_op jit(solution)/shard_map/ppermute | solution.py:33
  156.0 10.5 collective-permute-start.5
  321.9 15.0 collective-permute-start.6
  322.7 15.2 collective-permute-start.7
  327.5 5.6 collective-permute-start.8
  331.2 5.1 collective-permute-start.9
  490.7 16.1 collective-permute-start.10
  490.8 16.1 collective-permute-start.11
  496.6 8.8 collective-permute-start.12
  500.7 5.4 collective-permute-start.13
  662.5 15.7 collective-permute-start.14
  662.6 15.7 collective-permute-start.15
  668.4 8.4 collective-permute-start.16
  672.2 5.2 collective-permute-start.17
  835.8 15.8 collective-permute-start.18
  836.5 15.9 collective-permute-start.19
  842.2 7.7 collective-permute-start.20
  845.9 5.1 collective-permute-start.21
  1010.9 16.1 collective-permute-start.22
  1011.7 16.1 collective-permute-start.23
  1017.4 7.6 collective-permute-start.24
  1021.2 5.1 collective-permute-start.25
  1188.5 15.9 collective-permute-start.26
  1189.3 16.0 collective-permute-start.27
  1195.0 6.5 collective-permute-start.28
  1366.7 14.9 collective-permute-start.30
  1367.0 14.8 collective-permute-start.31
  1372.7 7.2 collective-permute-start.32
  (93 other events, 1334.6 us)
where the time goes:
time: 1630 us; the launch traced here: 1610 us
  blocking collectives  1090 us (67%)
  matrix products  178 us (11%)
  other arithmetic  138 us (8%)
  local copies, waits for them, and re-layouts  118 us (7%)
  starting transfers between devices  83.3 us (5%)
    psum x8, blocking collectives, per_device(): lax.psum(inner_local(image_block, image_block), ('lat', 'dep'))  511 us
    psum x8, blocking collectives, per_device(): coef_stack = lax.psum(local_prods, ('lat', 'dep'))  505 us
    psum x1, blocking collectives, per_device(): lax.psum(inner_local(rhs, rhs), ('lat', 'dep'))  68.8 us
    ppermute x16, starting transfers between devices, with_halo(): lax.ppermute(head, axis, [((i + 1) % count, i) for i in range(ends)])  54.5 us
    dot_general x52, matrix products, combine_columns(): return jnp.einsum('aevu,vw->aewu', vectors, matrix, precision=highest)  46.2 us
    another operation x7, other arithmetic, per_device(): jnp.linalg.cholesky(gram_small)  35.7 us
    dot_general x8, matrix products, apply_operator(): jnp.einsum('aeki,aevk->aevi', couple, near_traces, precision=highest)  34.6 us
    dot_general x8, matrix products, apply_operator(): jnp.einsum('aeij,aevj->aevi', diag_tiles, vectors, precision=highest)  33.2 us
  transfers between devices with their start and end apart: 34, of which 5 were waited for; matrix products, arithmetic and copies ran while one was open for 7% of the time, Pallas kernels for 0%

commit v1 on v0

v1 whole, which is shorter than its diff:
```python
import functools

import jax
import jax.numpy as jnp
from jax import lax
from jax.experimental import pallas as pl
from jax.experimental.pallas import tpu as pltpu
from jax.sharding import PartitionSpec as P

MESH = pl.DeviceIdType.MESH
highest = lax.Precision.HIGHEST
f32 = jnp.float32
bf16 = jnp.bfloat16

A_ROWS, E_ROWS = 4, 8
ELEMS = A_ROWS * E_ROWS
NV = 32
LANES = (128, 256, 256, 384)
ROWS = (128, 64, 64, 64)

NN = (((1,), (0,)), ((), ()))
NT = (((1,), (1,)), ((), ()))


def split(x):
    hi = x.astype(bf16)
    return hi, (x - hi.astype(f32)).astype(bf16)


def dot(a, b, dims=NN):
    return lax.dot_general(a, b, dims, preferred_element_type=f32)


def dot_exact(a, b, dims=NN):
    return lax.dot_general(a, b, dims, precision=highest, preferred_element_type=f32)


def dot3(ah, al, bh, bl, dims=NN):
    rows = ah.shape[0]
    both = dot(jnp.concatenate([ah, al], axis=0), bh, dims)
    return both[:rows] + both[rows:] + dot(ah, bl, dims)


def iota(shape, dim):
    return lax.broadcasted_iota(jnp.int32, shape, dim)


def eye(n):
    return (iota((n, n), 0) == iota((n, n), 1)).astype(f32)


def eliminate(gram):
    n = gram.shape[0]
    wide = jnp.concatenate([gram, eye(n)], axis=1)
    width = 2 * n
    row = iota((n, width), 0)
    for k in range(n - 1):
        column = jnp.broadcast_to(wide[:, k : k + 1], (n, width))
        pivot = column[k : k + 1, :]
        scaled = wide[k : k + 1, :] * (1.0 / pivot)
        wide = wide - jnp.where(row > k, column, 0.0) * scaled
    diag = jnp.sum(jnp.where(row == iota((n, width), 1), wide, 0.0), axis=1, keepdims=True)
    wide = wide * lax.rsqrt(diag)
    upper = jnp.where(iota((n, n), 0) <= iota((n, n), 1), wide[:, :n], 0.0)
    return upper, wide[:, n:]


def kernel(
    n_lat,
    n_dep,
    kappa_ref,
    state_ref,
    rate_ref,
    gt_ref,
    ga_ref,
    gb_ref,
    m_ref,
    rhs_ref,
    out_ref,
    basis_hi,
    basis_lo,
    stiff_hi,
    stiff_lo,
    field_a,
    field_b,
    own,
    kappa_pad,
    kappa_x,
    kappa_z,
    diag,
    cross,
    m_hi,
    m_lo,
    halo_out,
    halo_in,
    hess,
    nfac,
    ninv,
    ysol,
    sums,
    take_a,
    part,
    take_b,
    total,
    halo_send,
    halo_recv,
    a_send,
    a_recv,
    b_send,
    b_recv,
    c_send,
    c_recv,
):
    lat = lax.axis_index("lat")
    dep = lax.axis_index("dep")

    barrier = pltpu.get_barrier_semaphore()
    for k in range(1, n_dep):
        pl.semaphore_signal(
            barrier, inc=1, device_id=(lat, lax.rem(dep + k, n_dep)), device_id_type=MESH
        )
    for k in range(1, n_lat):
        pl.semaphore_signal(
            barrier, inc=1, device_id=(lax.rem(lat + k, n_lat), dep), device_id_type=MESH
        )

    lane = iota((1, 128), 1)
    node_x = lane % 64 // 16
    node_z = lane % 4

    kappa = kappa_ref[...]
    lanes32 = iota((ELEMS, 128), 1)
    edge_x = (lanes32 % 64 // 16 == 0) | (lanes32 % 64 // 16 == 3)
    edge_z = (lanes32 % 4 == 0) | (lanes32 % 4 == 3)
    touches = edge_x.astype(f32) + edge_z.astype(f32)
    diag[...] = 0.25 + kappa * touches
    cross[...] = rate_ref[...] * pltpu.roll(state_ref[...], 64, 1)
    kappa_x[...] = pltpu.roll(kappa, 80, 1)
    kappa_z[...] = pltpu.roll(kappa, 125, 1)
    kappa_pad[...] = jnp.ones_like(kappa_pad)
    for a in range(A_ROWS):
        base = (a + 1) * 10 + 1
        kappa_pad[base : base + E_ROWS, :] = kappa[a * E_ROWS : (a + 1) * E_ROWS, :]
    mh, ml = split(m_ref[...])
    m_hi[...] = mh
    m_lo[...] = ml
    for k in range(A_ROWS):
        for side in (0, E_ROWS + 1):
            field_a[(k + 1) * 10 + side] = jnp.zeros((NV, 128), f32)
            field_b[(k + 1) * 10 + side] = jnp.zeros((NV, 128), f32)

    def padded(el):
        return (el // E_ROWS + 1) * 10 + el % E_ROWS + 1

    @pl.loop(0, ELEMS)
    def _(el):
        row = kappa_ref[pl.ds(el, 1), :]
        turned = pltpu.roll(row, 64, 1)
        first = jnp.where(lane < 64, row, turned)
        second = jnp.where(lane < 64, turned, row)
        first = jnp.concatenate([first, first], axis=1)
        second = jnp.concatenate([second, second], axis=1)
        upper = dot_exact(gt_ref[...] * first, ga_ref[...])
        lower = dot_exact(gt_ref[...] * second, gb_ref[...])
        sh, sl = split(jnp.concatenate([upper, lower], axis=0))
        stiff_hi[el] = sh
        stiff_lo[el] = sl
        v = rhs_ref[el]
        vh, vl = split(v)
        basis_hi[el, 0:NV, :] = vh
        basis_lo[el, 0:NV, :] = vl
        field_a[padded(el)] = v

    pl.semaphore_wait(barrier, n_lat + n_dep - 2)

    def halo_copies(slot):
        right, left = lax.rem(lat + 1, n_lat), lax.rem(lat + n_lat - 1, n_lat)
        copies = []
        for index, (start, size, where) in enumerate(
            (
                (0, 2, (right, dep)),
                (2, 2, (left, dep)),
                (4, 1, (lat, lax.rem(dep + 1, n_dep))),
                (5, 1, (lat, lax.rem(dep + n_dep - 1, n_dep))),
            )
        ):
            copies.append(
                pltpu.make_async_remote_copy(
                    src_ref=halo_out.at[slot, pl.ds(start, size)],
                    dst_ref=halo_in.at[slot, pl.ds(start, size)],
                    send_sem=halo_send.at[slot, index],
                    recv_sem=halo_recv.at[slot, index],
                    device_id=where,
                    device_id_type=MESH,
                )
            )
        return copies

    has_above = dep < n_dep - 1
    has_below = dep > 0

    def operator(field, field_out, slot_in, slot_out, shift, parity):
        for p in range(2):
            right = None
            left = None
            for k in range(4):
                e = 4 * p + k
                index = 4 * 10 + e + 1
                there = pltpu.roll(
                    field[index] * kappa_pad[index : index + 1, :], (80 + 16 * k) % 128, 1
                )
                back = pltpu.roll(field[10 + e + 1], 16 * k, 1)
                mask = node_x == k
                right = there if right is None else jnp.where(mask, there, right)
                left = back if left is None else jnp.where(mask, back, left)
            halo_out[parity, p] = right
            halo_out[parity, 2 + p] = left
        up = None
        down = None
        for k in range(A_ROWS):
            index = (k + 1) * 10 + E_ROWS
            there = pltpu.roll(
                field[index] * kappa_pad[index : index + 1, :], (125 + k) % 128, 1
            )
            back = pltpu.roll(field[(k + 1) * 10 + 1], k, 1)
            mask = node_z == k
            up = there if up is None else jnp.where(mask, there, up)
            down = back if down is None else jnp.where(mask, back, down)
        halo_out[parity, 4] = up
        halo_out[parity, 5] = down
        copies = halo_copies(parity)
        copies[0].start()
        copies[1].start()

        @pl.when(has_above)
        def _():
            copies[2].start()

        @pl.when(has_below)
        def _():
            copies[3].start()

        @pl.loop(0, ELEMS // 2)
        def _(pair):
            for half in range(2):
                el = pair * 2 + half
                xh = basis_hi[el, slot_in * NV : (slot_in + 1) * NV, :]
                xl = basis_lo[el, slot_in * NV : (slot_in + 1) * NV, :]
                x = field[padded(el)]
                z = x * cross[pl.ds(el, 1), :]
                y = dot3(xh, xl, stiff_hi[el], stiff_lo[el])
                here = diag[pl.ds(el, 1), :]
                if shift is not None:
                    here = here - shift
                own[el] = y + x * here + (z + pltpu.roll(z, 64, 1))

        copies[0].wait()
        copies[1].wait()

        @pl.when(has_above)
        def _():
            copies[2].wait_send()
            copies[3].wait_recv()

        @pl.when(has_below)
        def _():
            copies[3].wait_send()
            copies[2].wait_recv()

        for p in range(2):
            for k in range(4):
                e = 4 * p + k
                field[e + 1] = pltpu.roll(halo_in[parity, p], (48 - 16 * k) % 128, 1)
                field[5 * 10 + e + 1] = pltpu.roll(halo_in[parity, 2 + p], (128 - 16 * k) % 128, 1)

        @pl.when(has_below)
        def _():
            for k in range(A_ROWS):
                field[(k + 1) * 10] = pltpu.roll(halo_in[parity, 4], 3 - k, 1)

        @pl.when(has_above)
        def _():
            for k in range(A_ROWS):
                field[(k + 1) * 10 + E_ROWS + 1] = pltpu.roll(
                    halo_in[parity, 5], (128 - k) % 128, 1
                )

        @pl.loop(0, ELEMS // 4)
        def _(group):
            vectors = []
            for k in range(4):
                el = group * 4 + k
                at = padded(el)
                sideways = jnp.where(
                    node_x == 3,
                    kappa_pad[pl.ds(at - 10, 1), :] * field[at - 10],
                    kappa_x[pl.ds(el, 1), :] * field[at + 10],
                )
                upright = jnp.where(
                    node_z == 3,
                    kappa_pad[pl.ds(at - 1, 1), :] * field[at - 1],
                    kappa_z[pl.ds(el, 1), :] * field[at + 1],
                )
                vectors.append(jnp.concatenate([sideways, upright], axis=1))
            ch, cl = split(jnp.concatenate(vectors, axis=0))
            coupled = dot3(ch, cl, m_hi[...], m_lo[...])
            for k in range(4):
                el = group * 4 + k
                w = own[el] - coupled[k * NV : (k + 1) * NV]
                wh, wl = split(w)
                basis_hi[el, slot_out * NV : (slot_out + 1) * NV, :] = wh
                basis_lo[el, slot_out * NV : (slot_out + 1) * NV, :] = wl
                if field_out is not None:
                    field_out[padded(el)] = w

    def gram(step):
        first = 0 if step == 0 else 2 * step + 1
        stop = 2 * step + 3
        rows = (stop - first) * NV
        width = stop * NV

        def body(pair, acc):
            def both(ref, begin, end):
                return jnp.concatenate(
                    [ref[pair * 2, begin:end, :], ref[pair * 2 + 1, begin:end, :]], axis=1
                )

            wh = both(basis_hi, first * NV, stop * NV)
            wl = both(basis_lo, first * NV, stop * NV)
            bh = both(basis_hi, 0, stop * NV)
            bl = both(basis_lo, 0, stop * NV)
            return acc + dot3(wh, wl, bh, bl, NT)

        value = lax.fori_loop(0, ELEMS // 2, body, jnp.zeros((rows, width), f32))
        buffer = sums[step]
        spare = LANES[step] - width
        if spare:
            value = jnp.concatenate([value, jnp.zeros((rows, spare), f32)], axis=1)
        buffer[0:rows, :] = value
        if ROWS[step] > rows:
            buffer[rows:, :] = jnp.zeros((ROWS[step] - rows, LANES[step]), f32)

    def all_sum(step, work):
        size = ROWS[step] // n_dep
        mine = pl.ds(pl.multiple_of(dep * size, 8), size)
        copies_a = []
        for k in range(1, n_dep):
            to = lax.rem(dep + k, n_dep)
            copies_a.append(
                pltpu.make_async_remote_copy(
                    src_ref=sums[step].at[pl.ds(pl.multiple_of(to * size, 8), size)],
                    dst_ref=take_a[step].at[k],
                    send_sem=a_send.at[step, k],
                    recv_sem=a_recv.at[step, k],
                    device_id=(lat, to),
                    device_id_type=MESH,
                )
            )
            copies_a[-1].start()
        if work is not None:
            work()
        value = sums[step][mine, :]
        for k in range(1, n_dep):
            copies_a[k - 1].wait_recv()
            value = value + take_a[step][k]
        part[step][...] = value
        copies_b = []
        for k in range(1, n_lat):
            copies_b.append(
                pltpu.make_async_remote_copy(
                    src_ref=part[step],
                    dst_ref=take_b[step].at[lat],
                    send_sem=b_send.at[step, k],
                    recv_sem=b_recv.at[step, k],
                    device_id=(lax.rem(lat + k, n_lat), dep),
                    device_id_type=MESH,
                )
            )
            copies_b[-1].start()
        take_b[step][lat] = value
        for copy in copies_b:
            copy.wait_recv()
        value = take_b[step][0]
        for k in range(1, n_lat):
            value = value + take_b[step][k]
        total[step][mine, :] = value
        copies_c = []
        for k in range(1, n_dep):
            copies_c.append(
                pltpu.make_async_remote_copy(
                    src_ref=total[step].at[mine],
                    dst_ref=total[step].at[mine],
                    send_sem=c_send.at[step, k],
                    recv_sem=c_recv.at[step, k],
                    device_id=(lat, lax.rem(dep + k, n_dep)),
                    device_id_type=MESH,
                )
            )
            copies_c[-1].start()
        for copy in copies_c:
            copy.wait_recv()
        for copy in copies_a + copies_b + copies_c:
            copy.wait_send()
        return total[step][...]

    def mix(step, table):
        first = 0 if step == 0 else 2 * step + 1
        stop = 2 * step + 3
        th, tl = split(table)

        @pl.loop(0, ELEMS // 2)
        def _(pair):
            def both(ref):
                return jnp.concatenate(
                    [ref[pair * 2, 0 : stop * NV, :], ref[pair * 2 + 1, 0 : stop * NV, :]],
                    axis=1,
                )

            fresh = dot3(th, tl, both(basis_hi), both(basis_lo))
            fh, fl = split(fresh)
            for half in range(2):
                el = pair * 2 + half
                cut = slice(half * 128, half * 128 + 128)
                basis_hi[el, first * NV : stop * NV, :] = fh[:, cut]
                basis_lo[el, first * NV : stop * NV, :] = fl[:, cut]
                field_a[padded(el)] = fresh[-NV:, cut]

    def extend(step):
        new = hess[step * 64 : step * 64 + 64, :]
        rows = dot_exact(new, hess[0 : step * 64 + 64, :], NT)
        right = dot_exact(new[:, 0:NV], ninv[4, 0:NV, 0:NV], NT)
        pieces = []
        for i in range(step):
            block = rows[:, i * 64 : i * 64 + 64]
            for k in range(i):
                block = block - dot_exact(pieces[k], nfac[i, k], NT)
            block = dot_exact(block, ninv[i], NT)
            pieces.append(block)
            nfac[step, i] = block
            right = right - dot_exact(block, ysol[i])
        corner = rows[:, step * 64 : step * 64 + 64]
        for block in pieces:
            corner = corner - dot_exact(block, block, NT)
        _, inverse = eliminate(corner)
        ninv[step] = inverse
        ysol[step] = dot_exact(inverse, right)

    hess[...] = jnp.zeros_like(hess)

    operator(field_a, field_b, 0, 1, None, 0)
    operator(field_b, None, 1, 2, None, 1)
    gram(0)
    table = all_sum(0, None)[0:96, 0:96]
    upper, inverse = eliminate(table)
    mix(0, inverse)
    lower = upper.T
    ninv[4] = jnp.concatenate(
        [jnp.concatenate([lower[0:NV, 0:NV], jnp.zeros((NV, NV), f32)], axis=1), jnp.zeros((NV, 64), f32)],
        axis=0,
    )
    column0 = dot_exact(inverse[0:NV, 0:NV], lower[NV : 2 * NV, :])
    column1 = dot_exact(
        inverse[NV : 2 * NV, NV : 2 * NV],
        lower[2 * NV :, :] - dot_exact(lower[NV : 2 * NV, 0:NV], column0),
    )
    hess[0:NV, 0:96] = column0
    hess[NV : 2 * NV, 0:96] = column1
    shift = jnp.sum(
        jnp.sum(jnp.where(iota((NV, 96), 0) == iota((NV, 96), 1), column0, 0.0), axis=1, keepdims=True),
        axis=0,
        keepdims=True,
    ) * (1.0 / NV)

    for step in range(1, 4):
        known = 2 * step + 1
        operator(field_a, field_b, known - 1, known, shift, 0)
        operator(field_b, None, known, known + 1, shift, 1)
        gram(step)
        table = all_sum(step, functools.partial(extend, step - 1))
        prods = table[:, 0 : known * NV]
        corner = table[:, known * NV : known * NV + 64] - dot_exact(prods, prods, NT)
        upper, inverse = eliminate(corner)
        weights = jnp.concatenate([-dot_exact(inverse, prods), inverse], axis=1)
        if step < 3:
            mix(step, weights)
        lower = upper.T
        width = (known + 2) * NV
        coefs = jnp.concatenate([prods, lower], axis=1)
        place = iota((NV, width), 1) - iota((NV, width), 0)
        first = coefs[0:NV] + jnp.where(place == (known - 1) * NV, shift, 0.0)
        hess[2 * step * NV : 2 * step * NV + NV, 0:width] = first
        second = coefs[NV:] + shift * coefs[0:NV]
        second = second - dot_exact(
            prods[0:NV, :], hess[0 : known * NV, 0:width]
        )
        second = dot_exact(inverse[0:NV, 0:NV], second)
        hess[known * NV : known * NV + NV, 0:width] = second
    extend(3)

    answers = [None] * 4
    for i in range(3, -1, -1):
        value = ysol[i]
        for k in range(i + 1, 4):
            value = value - dot_exact(nfac[k, i].T, answers[k])
        answers[i] = dot_exact(ninv[i].T, value)
    solved = jnp.concatenate(answers, axis=0).T
    final = solved[:, 7 * NV : 8 * NV]
    head = solved[:, 0 : 7 * NV] + dot_exact(final, weights[0:NV, 0 : 7 * NV])
    tail = dot_exact(final, weights[0:NV, 7 * NV : 8 * NV])
    th, tl = split(jnp.concatenate([head, tail], axis=1))

    @pl.loop(0, ELEMS // 2)
    def _(pair):
        def both(ref):
            return jnp.concatenate(
                [ref[pair * 2, 0 : 8 * NV, :], ref[pair * 2 + 1, 0 : 8 * NV, :]], axis=1
            )

        value = dot3(th, tl, both(basis_hi), both(basis_lo))
        out_ref[pair * 2] = value[:, 0:128]
        out_ref[pair * 2 + 1] = value[:, 128:256]


def solution(mesh):
    n_lat, n_dep = mesh.shape["lat"], mesh.shape["dep"]

    def per_device(state, kappa, rate, grads, lift, rhs):
        gt = jnp.concatenate([grads.transpose(2, 0, 1).reshape(64, 192), jnp.zeros((64, 64), f32)], axis=1)
        g = jnp.concatenate([grads.reshape(192, 64), jnp.zeros((64, 64), f32)], axis=0)
        zero = jnp.zeros_like(g)
        ga = jnp.concatenate([g, zero], axis=1)
        gb = jnp.concatenate([zero, g], axis=1)
        by_species = lift.reshape(4, 2, 16, 128)
        gap = jnp.zeros((2, 32, 128), f32)
        m_lat = jnp.concatenate([by_species[1], gap, by_species[0]], axis=1).reshape(128, 128)
        hole = jnp.zeros((32, 2, 128), f32)
        m_dep = jnp.concatenate([lift[3][:, None], hole, lift[2][:, None]], axis=1).reshape(128, 128)
        m = jnp.concatenate([m_lat, m_dep], axis=0)
        vmem = pl.BlockSpec(memory_space=pltpu.VMEM)
        V = pltpu.VMEM
        dma = pltpu.SemaphoreType.DMA
        out = pl.pallas_call(
            functools.partial(kernel, n_lat, n_dep),
            out_shape=jax.ShapeDtypeStruct((ELEMS, NV, 128), f32),
            in_specs=[vmem] * 8,
            out_specs=vmem,
            scratch_shapes=[
                V((ELEMS, 9 * NV, 128), bf16),
                V((ELEMS, 9 * NV, 128), bf16),
                V((ELEMS, 128, 128), bf16),
                V((ELEMS, 128, 128), bf16),
                V((60, NV, 128), f32),
                V((60, NV, 128), f32),
                V((ELEMS, NV, 128), f32),
                V((64, 128), f32),
                V((ELEMS, 128), f32),
                V((ELEMS, 128), f32),
                V((ELEMS, 128), f32),
                V((ELEMS, 128), f32),
                V((256, 128), bf16),
                V((256, 128), bf16),
                V((2, 6, NV, 128), f32),
                V((2, 6, NV, 128), f32),
                V((256, 384), f32),
                V((4, 4, 64, 64), f32),
                V((5, 64, 64), f32),
                V((4, 64, NV), f32),
                [V((ROWS[t], LANES[t]), f32) for t in range(4)],
                [V((n_dep, ROWS[t] // n_dep, LANES[t]), f32) for t in range(4)],
                [V((ROWS[t] // n_dep, LANES[t]), f32) for t in range(4)],
                [V((n_lat, ROWS[t] // n_dep, LANES[t]), f32) for t in range(4)],
                [V((ROWS[t], LANES[t]), f32) for t in range(4)],
                dma((2, 4)),
                dma((2, 4)),
                dma((4, n_dep)),
                dma((4, n_dep)),
                dma((4, n_lat)),
                dma((4, n_lat)),
                dma((4, n_dep)),
                dma((4, n_dep)),
            ],
            compiler_params=pltpu.CompilerParams(
                collective_id=0, has_side_effects=True, vmem_limit_bytes=60 * 1024 * 1024
            ),
        )(
            kappa.reshape(ELEMS, 128),
            state.reshape(ELEMS, 128),
            rate.reshape(ELEMS, 1),
            gt,
            ga,
            gb,
            m,
            rhs.reshape(ELEMS, NV, 128),
        )
        return out.reshape(A_ROWS, E_ROWS, NV, 128)

    in_specs = (
        P("lat", "dep", None),
        P("lat", "dep", None),
        P("lat", "dep"),
        P(),
        P(),
        P("lat", "dep", None, None),
    )
    return jax.shard_map(
        per_device, mesh=mesh, in_specs=in_specs, out_specs=P("lat", "dep", None, None), check_vma=False
    )
```

time: 1630 us -> 200 us (0.12)
  blocking collectives: 1090 us -> 0 us
  Pallas kernels: 0 us -> 193 us
  matrix products: 178 us -> 0 us
  other arithmetic: 138 us -> 0.92 us
  local copies, waits for them, and re-layouts: 118 us -> 5.86 us
  starting transfers between devices: 83.3 us -> 0 us
    psum x17 -> x0, blocking collectives: 1090 us -> none  [the longest x8 511 us: per_device(): lax.psum(inner_local(image_block, image_block), ('lat', 'dep'))]
    pallas_call x0 -> x1, Pallas kernels: none -> 193 us  [per_device(): pl.pallas_call(functools.partial(kernel, n_lat, n_dep), out_shape=jax.Sha...]
    dot_general x139 -> x0, matrix products: 171 us -> none  [the longest x52 46.2 us: combine_columns(): return jnp.einsum('aevu,vw->aewu', vectors, matrix, precision=highest)]
    another operation x54 -> x0, other arithmetic: 114 us -> none  [the longest x7 35.7 us: per_device(): jnp.linalg.cholesky(gram_small)]
    ppermute x34 -> x0, starting transfers between devices: 83.3 us -> none  [the longest x16 54.5 us: with_halo(): lax.ppermute(head, axis, [((i + 1) % count, i) for i in range(ends)])]
    slice x72 -> x1, local copies, waits for them, and re-layouts: 51.2 us -> 0.01 us  [per_device(): by_species[1]]
    another operation x41 -> x0, local copies, waits for them, and re-layouts: 28.6 us -> none  [the longest x8 6.7 us: apply_operator(): next_lat[None]]
  transfers between devices with their start and end apart: 34 -> 0, of which waited for: 5 -> 0; matrix products, arithmetic and copies ran while one was open for 7% -> 0% of each run, Pallas kernels for 0% -> 0%
where the time goes in v1:
time: 200 us
  Pallas kernels  193 us (96%)
  local copies, waits for them, and re-layouts  5.86 us (3%)
    pallas_call x1, Pallas kernels, per_device(): pl.pallas_call(functools.partial(kernel, n_lat, n_dep), out_shape=jax.Sha...  193 us

profile of v1, /device:TPU:1, one launch (start us, length us, event | category | flops | bytes accessed | tf_op | source)
XLA Modules:
  0.0 199.6 jit_solution(15592190608120377632)
XLA Ops:
  0.0 0.1 pad.10.clone
  0.1 0.0 copy-start.2
  0.1 0.1 pad.7.clone
  0.2 0.6 copy-done.2
  0.8 0.7 reshape.41.rate_ref
  1.4 1.0 copy.11
  2.4 0.0 copy-start.1
  2.4 0.6 concatenate.21.gt_ref
  3.1 0.2 copy-done.1
  3.3 0.0 copy-start
  3.3 0.1 pad_maximum_fusion.1
  3.3 0.1 pad_maximum_fusion.2
  3.4 0.7 copy-done
  4.2 0.8 fusion
  4.9 192.8 %shard_map.64 = f32[32,32,128]{2,1,0:T(8,128)} custom-call(f32[32,128]{1,0:T(8,128)} %bitcast.28, f32[32,128]{1,0:T(8,128)} %bitcast.29, f32[32,1]{1,0:T(8,128)} %reshape.41.rate_ref, f32[64,256]{1,0:T(8,128)} %concatenate.21.gt_ref, f32[256,128]{1,0:T(8,128)} %get-tuple-element.6.ga_ref, f32[256,128]{1,0:T(8,128)} %get-tuple-element.5.gb_ref, ...), custom_call_target="tpu_custom_call" | custom-call | tf_op jit(solution)/shard_map/pallas_call | solution.py:542
  197.8 1.9 copy.16
  (4 shorter events, 0.0 us)
Async XLA Ops:
  0.1 0.7 copy-start.2
  2.4 0.8 copy-start.1
  3.3 0.9 copy-start

commit v2 on v1

v2 whole, which is shorter than its diff:
```python
import functools

import jax
import jax.numpy as jnp
from jax import lax
from jax.experimental import pallas as pl
from jax.experimental.pallas import tpu as pltpu
from jax.sharding import PartitionSpec as P

MESH = pl.DeviceIdType.MESH
highest = lax.Precision.HIGHEST
f32 = jnp.float32
bf16 = jnp.bfloat16

A_ROWS, E_ROWS = 4, 8
ELEMS = A_ROWS * E_ROWS
OWN, PAIR, MIX = 16, 32, 8
NV = 32
STEPS = 3
RAW = 3 * NV
KNOWN = (0, 3, 6)
SUM_ROWS = (128, 192, 320)
CUTS = (0, 64, 160, 256)

NN = (((1,), (0,)), ((), ()))
NT = (((1,), (1,)), ((), ()))


def split(x):
    hi = x.astype(bf16)
    return hi, (x - hi.astype(f32)).astype(bf16)


def dot(a, b, dims=NN):
    return lax.dot_general(a, b, dims, preferred_element_type=f32)


def dot_exact(a, b, dims=NN):
    return lax.dot_general(a, b, dims, precision=highest, preferred_element_type=f32)


def dot3(ah, al, bh, bl, dims=NN):
    rows = ah.shape[0]
    both = dot(jnp.concatenate([ah, al], axis=0), bh, dims)
    return both[:rows] + both[rows:] + dot(ah, bl, dims)


def dot4(ah, al, bh, bl, dims=NN):
    rows = ah.shape[0]
    stacked = jnp.concatenate([ah, al], axis=0)
    high = dot(stacked, bh, dims)
    low = dot(stacked, bl, dims)
    return high[:rows] + (high[rows:] + (low[:rows] + low[rows:]))


def iota(shape, dim):
    return lax.broadcasted_iota(jnp.int32, shape, dim)


def eye(n):
    return (iota((n, n), 0) == iota((n, n), 1)).astype(f32)


class Elimination:
    def __init__(self, gram):
        self.n = gram.shape[0]
        wide = jnp.concatenate([gram, eye(self.n)], axis=1)
        self.tiles = [wide[8 * i : 8 * i + 8] for i in range(self.n // 8)]

    def run(self, begin, end):
        width = 2 * self.n
        row = iota((8, width), 0)

        def column(x, k):
            return jnp.broadcast_to(x[:, k : k + 1], (8, width))

        for k in range(begin, end, 2):
            p, q = k // 8, k % 8
            x = self.tiles[p]
            head0, head1 = column(x, k), column(x, k + 1)
            row0, row1 = x[q : q + 1, :], x[q + 1 : q + 2, :]
            a, b, c = head0[q : q + 1], head1[q : q + 1], head1[q + 1 : q + 2]
            a_inv = 1.0 / a
            det_inv = 1.0 / (a * c - b * b)
            t = b * a_inv
            scaled0 = row0 * a_inv
            scaled1 = (row1 - t * row0) * (a * det_inv)
            for i in range(p, self.n // 8):
                x = self.tiles[i]
                c0 = head0 if i == p else column(x, k)
                c1 = head1 if i == p else column(x, k + 1)
                c1 = c1 - c0 * t
                if i == p:
                    c0 = jnp.where(row > q, c0, 0.0)
                    c1 = jnp.where(row > q + 1, c1, 0.0)
                self.tiles[i] = x - c0 * scaled0 - c1 * scaled1

    def finish(self):
        n, width = self.n, 2 * self.n
        wide = jnp.concatenate(self.tiles, axis=0)
        on_diag = iota((n, width), 0) == iota((n, width), 1)
        pivots = jnp.sum(jnp.where(on_diag, wide, 0.0), axis=1, keepdims=True)
        wide = wide * lax.rsqrt(pivots)
        upper = jnp.where(iota((n, n), 0) <= iota((n, n), 1), wide[:, :n], 0.0)
        return upper, wide[:, n:]


def eliminate(gram):
    work = Elimination(gram)
    work.run(0, work.n)
    return work.finish()


def kernel(
    n_lat,
    n_dep,
    kappa_ref,
    state_ref,
    rate_ref,
    grads_ref,
    lift_ref,
    rhs_ref,
    out_ref,
    basis_hi,
    basis_lo,
    stiff_hi,
    stiff_lo,
    field_a,
    field_b,
    own,
    kappa_pad,
    kappa_x,
    kappa_z,
    diag,
    cross,
    m_hi,
    m_lo,
    halo_out,
    halo_in,
    hess,
    start,
    nfac,
    ninv,
    ysol,
    sums,
    take_a,
    part,
    take_b,
    total,
    halo_send,
    halo_recv,
    a_send,
    a_recv,
    b_send,
    b_recv,
    c_send,
    c_recv,
):
    lat = lax.axis_index("lat")
    dep = lax.axis_index("dep")

    barrier = pltpu.get_barrier_semaphore()
    for k in range(1, n_dep):
        pl.semaphore_signal(
            barrier, inc=1, device_id=(lat, lax.rem(dep + k, n_dep)), device_id_type=MESH
        )
    for k in range(1, n_lat):
        pl.semaphore_signal(
            barrier, inc=1, device_id=(lax.rem(lat + k, n_lat), dep), device_id_type=MESH
        )

    lane = iota((1, 128), 1)
    node_x = lane % 64 // 16
    node_z = lane % 4

    def padded(el):
        return (el // E_ROWS + 1) * 10 + el % E_ROWS + 1

    touches = (node_x == 0) | (node_x == 3)
    touches = touches.astype(f32) + ((node_z == 0) | (node_z == 3)).astype(f32)
    kappa_pad[...] = jnp.ones_like(kappa_pad)
    for a in range(A_ROWS):
        here = slice(a * E_ROWS, (a + 1) * E_ROWS)
        kappa = kappa_ref[a]
        picked = iota((E_ROWS, E_ROWS), 0) == iota((E_ROWS, E_ROWS), 1)
        speed = jnp.sum(jnp.where(picked, rate_ref[a : a + 1, :], 0.0), axis=1, keepdims=True)
        diag[here, :] = 0.25 + kappa * touches
        cross[here, :] = speed * pltpu.roll(state_ref[a], 64, 1)
        kappa_x[here, :] = pltpu.roll(kappa, 80, 1)
        kappa_z[here, :] = pltpu.roll(kappa, 125, 1)
        base = (a + 1) * 10 + 1
        kappa_pad[base : base + E_ROWS, :] = kappa
        for side in (0, E_ROWS + 1):
            field_a[(a + 1) * 10 + side] = jnp.zeros((NV, 128), f32)
            field_b[(a + 1) * 10 + side] = jnp.zeros((NV, 128), f32)

    for a in range(A_ROWS):
        for e in range(E_ROWS):
            el = a * E_ROWS + e
            v = rhs_ref[a, e]
            vh, vl = split(v)
            basis_hi[el, 0:NV, :] = vh
            basis_lo[el, 0:NV, :] = vl
            field_a[padded(el)] = v

    def halo_copies(slot):
        right, left = lax.rem(lat + 1, n_lat), lax.rem(lat + n_lat - 1, n_lat)
        copies = []
        for index, (start, size, where) in enumerate(
            (
                (0, 2, (right, dep)),
                (2, 2, (left, dep)),
                (4, 1, (lat, lax.rem(dep + 1, n_dep))),
                (5, 1, (lat, lax.rem(dep + n_dep - 1, n_dep))),
            )
        ):
            copies.append(
                pltpu.make_async_remote_copy(
                    src_ref=halo_out.at[slot, pl.ds(start, size)],
                    dst_ref=halo_in.at[slot, pl.ds(start, size)],
                    send_sem=halo_send.at[slot, index],
                    recv_sem=halo_recv.at[slot, index],
                    device_id=where,
                    device_id_type=MESH,
                )
            )
        return copies

    has_above = dep < n_dep - 1
    has_below = dep > 0

    def send_faces(field, parity):
        for p in range(2):
            right = None
            left = None
            for k in range(4):
                e = 4 * p + k
                index = 4 * 10 + e + 1
                there = pltpu.roll(
                    field[index] * kappa_pad[index : index + 1, :], (80 + 16 * k) % 128, 1
                )
                back = pltpu.roll(field[10 + e + 1], 16 * k, 1)
                mask = node_x == k
                right = there if right is None else jnp.where(mask, there, right)
                left = back if left is None else jnp.where(mask, back, left)
            halo_out[parity, p] = right
            halo_out[parity, 2 + p] = left
        up = None
        down = None
        for k in range(A_ROWS):
            index = (k + 1) * 10 + E_ROWS
            there = pltpu.roll(
                field[index] * kappa_pad[index : index + 1, :], (125 + k) % 128, 1
            )
            back = pltpu.roll(field[(k + 1) * 10 + 1], k, 1)
            mask = node_z == k
            up = there if up is None else jnp.where(mask, there, up)
            down = back if down is None else jnp.where(mask, back, down)
        halo_out[parity, 4] = up
        halo_out[parity, 5] = down
        copies = halo_copies(parity)
        copies[0].start()
        copies[1].start()

        @pl.when(has_above)
        def _():
            copies[2].start()

        @pl.when(has_below)
        def _():
            copies[3].start()

        return copies

    def operator(field, field_out, slot_in, slot_out, shift, parity, copies):
        @pl.loop(0, ELEMS // OWN)
        def _(group):
            for k in range(OWN):
                el = group * OWN + k
                xh = basis_hi[el, slot_in * NV : (slot_in + 1) * NV, :]
                xl = basis_lo[el, slot_in * NV : (slot_in + 1) * NV, :]
                x = field[padded(el)]
                z = x * cross[pl.ds(el, 1), :]
                y = dot3(xh, xl, stiff_hi[el], stiff_lo[el])
                here = diag[pl.ds(el, 1), :]
                if shift is not None:
                    here = here - shift
                own[el] = y + x * here + (z + pltpu.roll(z, 64, 1))

        copies[0].wait()
        copies[1].wait()

        @pl.when(has_above)
        def _():
            copies[2].wait_send()
            copies[3].wait_recv()

        @pl.when(has_below)
        def _():
            copies[3].wait_send()
            copies[2].wait_recv()

        for p in range(2):
            for k in range(4):
                e = 4 * p + k
                field[e + 1] = pltpu.roll(halo_in[parity, p], (48 - 16 * k) % 128, 1)
                field[5 * 10 + e + 1] = pltpu.roll(halo_in[parity, 2 + p], (128 - 16 * k) % 128, 1)

        @pl.when(has_below)
        def _():
            for k in range(A_ROWS):
                field[(k + 1) * 10] = pltpu.roll(halo_in[parity, 4], 3 - k, 1)

        @pl.when(has_above)
        def _():
            for k in range(A_ROWS):
                field[(k + 1) * 10 + E_ROWS + 1] = pltpu.roll(
                    halo_in[parity, 5], (128 - k) % 128, 1
                )

        @pl.loop(0, ELEMS // PAIR)
        def _(bunch):
            for part_of in range(PAIR // 4):
                vectors = []
                for k in range(4):
                    el = bunch * PAIR + part_of * 4 + k
                    at = padded(el)
                    sideways = jnp.where(
                        node_x == 3,
                        kappa_pad[pl.ds(at - 10, 1), :] * field[at - 10],
                        kappa_x[pl.ds(el, 1), :] * field[at + 10],
                    )
                    upright = jnp.where(
                        node_z == 3,
                        kappa_pad[pl.ds(at - 1, 1), :] * field[at - 1],
                        kappa_z[pl.ds(el, 1), :] * field[at + 1],
                    )
                    vectors.append(jnp.concatenate([sideways, upright], axis=1))
                ch, cl = split(jnp.concatenate(vectors, axis=0))
                coupled = dot3(ch, cl, m_hi[...], m_lo[...])
                for k in range(4):
                    el = bunch * PAIR + part_of * 4 + k
                    w = own[el] - coupled[k * NV : (k + 1) * NV]
                    wh, wl = split(w)
                    basis_hi[el, slot_out * NV : (slot_out + 1) * NV, :] = wh
                    basis_lo[el, slot_out * NV : (slot_out + 1) * NV, :] = wl
                    if field_out is not None:
                        field_out[padded(el)] = w

    def gram(step):
        first = KNOWN[step] * NV
        stop = first + RAW

        def body(quad, acc):
            def four(ref, begin, end):
                return jnp.concatenate([ref[quad * 4 + k, begin:end, :] for k in range(4)], axis=1)

            wh, wl = four(basis_hi, first, stop), four(basis_lo, first, stop)
            bh, bl = four(basis_hi, 0, stop), four(basis_lo, 0, stop)
            return acc + dot4(wh, wl, bh, bl, NT)

        value = lax.fori_loop(0, ELEMS // 4, body, jnp.zeros((RAW, stop), f32))
        for i in range(step + 1):
            piece = value[:, i * 128 : min(i * 128 + 128, stop)]
            spare = 128 - piece.shape[1]
            if spare:
                piece = jnp.concatenate([piece, jnp.zeros((RAW, spare), f32)], axis=1)
            sums[step][i * RAW : (i + 1) * RAW, :] = piece
        used = (step + 1) * RAW
        if SUM_ROWS[step] > used:
            sums[step][used:, :] = jnp.zeros((SUM_ROWS[step] - used, 128), f32)

    def all_sum(step, work):
        size = SUM_ROWS[step] // n_dep
        mine = pl.ds(pl.multiple_of(dep * size, 8), size)
        copies_a = []
        for k in range(1, n_dep):
            to = lax.rem(dep + k, n_dep)
            copies_a.append(
                pltpu.make_async_remote_copy(
                    src_ref=sums[step].at[pl.ds(pl.multiple_of(to * size, 8), size)],
                    dst_ref=take_a[step].at[k],
                    send_sem=a_send.at[step, k],
                    recv_sem=a_recv.at[step, k],
                    device_id=(lat, to),
                    device_id_type=MESH,
                )
            )
            copies_a[-1].start()
        work(0)
        value = sums[step][mine, :]
        for k in range(1, n_dep):
            copies_a[k - 1].wait_recv()
            value = value + take_a[step][k]
        part[step][...] = value
        copies_b = []
        for k in range(1, n_lat):
            copies_b.append(
                pltpu.make_async_remote_copy(
                    src_ref=part[step],
                    dst_ref=take_b[step].at[lat],
                    send_sem=b_send.at[step, k],
                    recv_sem=b_recv.at[step, k],
                    device_id=(lax.rem(lat + k, n_lat), dep),
                    device_id_type=MESH,
                )
            )
            copies_b[-1].start()
        take_b[step][lat] = value
        work(1)
        for copy in copies_b:
            copy.wait_recv()
        value = take_b[step][0]
        for k in range(1, n_lat):
            value = value + take_b[step][k]
        total[step][mine, :] = value
        copies_c = []
        for k in range(1, n_dep):
            copies_c.append(
                pltpu.make_async_remote_copy(
                    src_ref=total[step].at[mine],
                    dst_ref=total[step].at[mine],
                    send_sem=c_send.at[step, k],
                    recv_sem=c_recv.at[step, k],
                    device_id=(lat, lax.rem(dep + k, n_dep)),
                    device_id_type=MESH,
                )
            )
            copies_c[-1].start()
        work(2)
        for copy in copies_c:
            copy.wait_recv()
        for copy in copies_a + copies_b + copies_c:
            copy.wait_send()
        return jnp.concatenate(
            [total[step][i * RAW : (i + 1) * RAW, :] for i in range(step + 1)], axis=1
        )

    def mix(step, table):
        first = KNOWN[step] * NV
        stop = first + RAW
        th, tl = split(table)

        @pl.loop(0, ELEMS // MIX)
        def _(bunch):
            for k in range(0, MIX, 2):
                el = bunch * MIX + k

                def both(ref):
                    return jnp.concatenate([ref[el, 0:stop, :], ref[el + 1, 0:stop, :]], axis=1)

                fresh = dot3(th, tl, both(basis_hi), both(basis_lo))
                fh, fl = split(fresh)
                for half in range(2):
                    cut = slice(half * 128, half * 128 + 128)
                    basis_hi[el + half, first:stop, :] = fh[:, cut]
                    basis_lo[el + half, first:stop, :] = fl[:, cut]
                    field_a[padded(el + half)] = fresh[-NV:, cut]

    def extend(step, metric=None):
        begin, end = CUTS[step], CUTS[step + 1]
        size = end - begin
        state = {}

        def products():
            new = hess[begin:end, :]
            if metric is None:
                rows = dot_exact(new, hess[0:end, :], NT)
            else:
                rows = dot_exact(new[:, 0:192], hess[0:end, 0:192], NT)
            right = dot_exact(new[:, 0:NV], start[...], NT)
            corner = rows[:, begin:end]
            if metric is not None:
                corner = corner + metric
            pieces = []
            for i in range(step):
                block = rows[:, CUTS[i] : CUTS[i + 1]]
                for k in range(i):
                    block = block - dot_exact(pieces[k], nfac[(i, k)][...], NT)
                block = dot_exact(block, ninv[i][...], NT)
                pieces.append(block)
                nfac[(step, i)][...] = block
                right = right - dot_exact(block, ysol[i][...])
            for block in pieces:
                corner = corner - dot_exact(block, block, NT)
            state["right"] = right
            state["work"] = Elimination(corner)

        def last():
            _, inverse = state["work"].finish()
            ninv[step][...] = inverse
            ysol[step][...] = dot_exact(inverse, state["right"])

        def run(stage):
            first, second = size // 4 // 2 * 2, size * 3 // 4 // 2 * 2
            if stage == 0:
                products()
                state["work"].run(0, first)
            elif stage == 1:
                state["work"].run(first, second)
            else:
                state["work"].run(second, size)
                last()

        return run

    def idle(stage):
        if stage == 0:
            hess[...] = jnp.zeros_like(hess)

    pl.semaphore_wait(barrier, n_lat + n_dep - 2)
    copies = send_faces(field_a, 0)

    g = jnp.concatenate([grads_ref[0], grads_ref[1], grads_ref[2], jnp.zeros((64, 64), f32)], axis=0)
    gt = g.T
    gh, gl = split(jnp.concatenate([g, g], axis=1))
    same = (iota((128, 128), 0) < 64) == (iota((128, 128), 1) < 64)
    low_lanes = lane < 64
    none = jnp.zeros((32, 128), f32)
    m_lat = []
    for s in range(2):
        at = slice(s * 16, s * 16 + 16)
        m_lat += [lift_ref[1, at, :], none, lift_ref[0, at, :]]
    place = iota((128, 32), 0) - 4 * iota((128, 32), 1)
    m_dep = dot_exact((place == 3).astype(f32), lift_ref[2]) + dot_exact(
        (place == 0).astype(f32), lift_ref[3]
    )
    mh, ml = split(jnp.concatenate(m_lat + [m_dep], axis=0))
    m_hi[...] = mh
    m_lo[...] = ml

    @pl.loop(0, A_ROWS)
    def _(a):
        for two in range(E_ROWS // 4):
            scaled = []
            for k in range(4):
                row = kappa_ref[a, two * 4 + k : two * 4 + k + 1, :]
                turned = pltpu.roll(row, 64, 1)
                first = jnp.where(low_lanes, row, turned)
                second = jnp.where(low_lanes, turned, row)
                scaled.append(gt * jnp.concatenate([first, first], axis=1))
                scaled.append(gt * jnp.concatenate([second, second], axis=1))
            sh, sl = split(jnp.concatenate(scaled, axis=0))
            blocks = dot3(sh, sl, gh, gl)
            for k in range(4):
                block = jnp.where(same, blocks[k * 128 : (k + 1) * 128], 0.0)
                bh, bl = split(block)
                el = a * E_ROWS + two * 4 + k
                stiff_hi[el] = bh
                stiff_lo[el] = bl

    operator(field_a, field_b, 0, 1, None, 0, copies)
    copies = send_faces(field_b, 1)
    operator(field_b, None, 1, 2, None, 1, copies)
    gram(0)
    table = all_sum(0, idle)[:, 0:RAW]
    upper, inverse = eliminate(table)
    mix(0, inverse)
    copies = send_faces(field_a, 0)
    lower = upper.T
    start[...] = lower[0:NV, 0:NV]
    column0 = dot_exact(inverse[0:NV, 0:NV], lower[NV : 2 * NV, :])
    column1 = dot_exact(
        inverse[NV : 2 * NV, NV : 2 * NV],
        lower[2 * NV :, :] - dot_exact(lower[NV : 2 * NV, 0:NV], column0),
    )
    hess[0:NV, 0:RAW] = column0
    hess[NV : 2 * NV, 0:RAW] = column1
    on_diag = iota((NV, RAW), 0) == iota((NV, RAW), 1)
    shift = jnp.sum(
        jnp.sum(jnp.where(on_diag, column0, 0.0), axis=1, keepdims=True), axis=0, keepdims=True
    ) * (1.0 / NV)

    for step in (1, 2):
        known = KNOWN[step]
        base = known * NV
        width = base + RAW
        operator(field_a, field_b, known - 1, known, shift, 0, copies)
        copies = send_faces(field_b, 1)
        operator(field_b, field_a, known, known + 1, shift, 1, copies)
        copies = send_faces(field_a, 0)
        operator(field_a, None, known + 1, known + 2, shift, 0, copies)
        gram(step)
        table = all_sum(step, extend(step - 1))
        prods = table[:, 0:base]
        corner = table[:, base:width] - dot_exact(prods, prods, NT)
        if step == 1:
            upper, inverse = eliminate(corner)
            mix(step, jnp.concatenate([-dot_exact(inverse, prods), inverse], axis=1))
            copies = send_faces(field_a, 0)
            tail = upper.T
        else:
            tail = eye(RAW)
        coefs = jnp.concatenate([prods, tail], axis=1)
        place = iota((NV, width), 1) - iota((NV, width), 0)
        row = CUTS[step]
        hess[row : row + NV, 0:width] = coefs[0:NV] + jnp.where(place == base - NV, shift, 0.0)
        for k in (1, 2):
            at = slice(k * NV, (k + 1) * NV)
            before = slice((k - 1) * NV, k * NV)
            column = coefs[at] + shift * coefs[before]
            reach = base if step == 2 else base + (k - 1) * NV
            column = column - dot_exact(coefs[before, 0:reach], hess[0:reach, 0:width])
            if step == 1:
                column = dot_exact(inverse[before, before], column)
            hess[row + k * NV : row + (k + 1) * NV, 0:width] = column

    spread = hess[CUTS[2] : CUTS[3], 6 * NV : 9 * NV]
    last = extend(2, dot_exact(dot_exact(spread, corner), spread, NT))
    for stage in range(3):
        last(stage)

    answers = [None] * STEPS
    for i in range(STEPS - 1, -1, -1):
        value = ysol[i][...]
        for k in range(i + 1, STEPS):
            value = value - dot_exact(nfac[(k, i)][...].T, answers[k])
        answers[i] = dot_exact(ninv[i][...].T, value)
    solved = jnp.concatenate(answers, axis=0).T
    tail = solved[:, 6 * NV : 8 * NV]
    head = solved[:, 0 : 6 * NV] - dot_exact(tail, prods[0 : 2 * NV, :])
    th, tl = split(jnp.concatenate([head, tail], axis=1))

    @pl.loop(0, A_ROWS)
    def _(a):
        for k in range(0, E_ROWS, 2):
            el = a * E_ROWS + k

            def both(ref):
                return jnp.concatenate([ref[el, 0 : 8 * NV, :], ref[el + 1, 0 : 8 * NV, :]], axis=1)

            value = dot3(th, tl, both(basis_hi), both(basis_lo))
            out_ref[a, k] = value[:, 0:128]
            out_ref[a, k + 1] = value[:, 128:256]


def solution(mesh):
    n_lat, n_dep = mesh.shape["lat"], mesh.shape["dep"]

    def per_device(state, kappa, rate, grads, lift, rhs):
        vmem = pl.BlockSpec(memory_space=pltpu.VMEM)
        V = pltpu.VMEM
        dma = pltpu.SemaphoreType.DMA
        out = pl.pallas_call(
            functools.partial(kernel, n_lat, n_dep),
            out_shape=jax.ShapeDtypeStruct((A_ROWS, E_ROWS, NV, 128), f32),
            in_specs=[vmem] * 6,
            out_specs=vmem,
            scratch_shapes=[
                V((ELEMS, 9 * NV, 128), bf16),
                V((ELEMS, 9 * NV, 128), bf16),
                V((ELEMS, 128, 128), bf16),
                V((ELEMS, 128, 128), bf16),
                V((60, NV, 128), f32),
                V((60, NV, 128), f32),
                V((ELEMS, NV, 128), f32),
                V((64, 128), f32),
                V((ELEMS, 128), f32),
                V((ELEMS, 128), f32),
                V((ELEMS, 128), f32),
                V((ELEMS, 128), f32),
                V((256, 128), bf16),
                V((256, 128), bf16),
                V((2, 6, NV, 128), f32),
                V((2, 6, NV, 128), f32),
                V((256, 384), f32),
                V((NV, NV), f32),
                {
                    (i, k): V((CUTS[i + 1] - CUTS[i], CUTS[k + 1] - CUTS[k]), f32)
                    for i in range(STEPS)
                    for k in range(i)
                },
                [V((CUTS[i + 1] - CUTS[i], CUTS[i + 1] - CUTS[i]), f32) for i in range(STEPS)],
                [V((CUTS[i + 1] - CUTS[i], NV), f32) for i in range(STEPS)],
                [V((rows, 128), f32) for rows in SUM_ROWS],
                [V((n_dep, rows // n_dep, 128), f32) for rows in SUM_ROWS],
                [V((rows // n_dep, 128), f32) for rows in SUM_ROWS],
                [V((n_lat, rows // n_dep, 128), f32) for rows in SUM_ROWS],
                [V((rows, 128), f32) for rows in SUM_ROWS],
                dma((2, 4)),
                dma((2, 4)),
                dma((STEPS, n_dep)),
                dma((STEPS, n_dep)),
                dma((STEPS, n_lat)),
                dma((STEPS, n_lat)),
                dma((STEPS, n_dep)),
                dma((STEPS, n_dep)),
            ],
            compiler_params=pltpu.CompilerParams(
                collective_id=0, has_side_effects=True, vmem_limit_bytes=60 * 1024 * 1024
            ),
        )(
            kappa, state, rate, grads, lift, rhs
        )
        return out

    in_specs = (
        P("lat", "dep", None),
        P("lat", "dep", None),
        P("lat", "dep"),
        P(),
        P(),
        P("lat", "dep", None, None),
    )
    return jax.shard_map(
        per_device, mesh=mesh, in_specs=in_specs, out_specs=P("lat", "dep", None, None), check_vma=False
    )
```

time: 200 us -> 130 us (0.65)
  Pallas kernels: 193 us -> 128 us
  local copies, waits for them, and re-layouts: 5.86 us -> 1.87 us
    pallas_call x1, Pallas kernels: 193 us -> 128 us  [per_device(): pl.pallas_call(functools.partial(kernel, n_lat, n_dep), out_shape=jax.Sha...]
where the time goes in v2:
time: 130 us
  Pallas kernels  128 us (98%)
  local copies, waits for them, and re-layouts  1.87 us (1%)
    pallas_call x1, Pallas kernels, per_device(): pl.pallas_call(functools.partial(kernel, n_lat, n_dep), out_shape=jax.Sha...  128 us

profile of v2, /device:TPU:1, one launch (start us, length us, event | category | flops | bytes accessed | tf_op | source)
XLA Modules:
  0.0 130.0 jit_solution(13370802953828915813)
XLA Ops:
  0.0 128.1 %shard_map.64 = f32[4,8,32,128]{3,2,1,0:T(8,128)} custom-call(f32[4,8,128]{2,1,0:T(8,128)} %kappa_ref.1, f32[4,8,128]{2,1,0:T(8,128)} %state_ref.1, f32[4,8]{1,0:T(4,128)} %rate_ref.1, f32[3,64,64]{2,1,0:T(8,128)} %grads_ref.1, f32[4,32,128]{2,1,0:T(8,128)} %lift_ref.1, f32[4,8,32,128]{3,2,1,0:T(8,128)} %rhs_ref.1), custom_call_target="tpu_custom_call" | custom-call | tf_op jit(solution)/shard_map/pallas_call | solution.py:644
  128.1 1.9 %copy.8 = f32[4,8,32,128]{3,2,1,0:T(8,128)} copy(f32[4,8,32,128]{3,2,1,0:T(8,128)} %shard_map.64) | data formatting | bytes 1048576

commit v3 on v2

--- a/solution.py
+++ b/solution.py
@@ -14,7 +14,8 @@
 
 A_ROWS, E_ROWS = 4, 8
 ELEMS = A_ROWS * E_ROWS
-OWN, PAIR, MIX = 16, 32, 8
+OWN, PAIR, MIX = 32, 32, 8
+FACES = 6
 NV = 32
 STEPS = 3
 RAW = 3 * NV
@@ -137,6 +138,7 @@
     m_lo,
     halo_out,
     halo_in,
+    halo_mix,
     hess,
     start,
     nfac,
@@ -194,6 +196,9 @@
             field_a[(a + 1) * 10 + side] = jnp.zeros((NV, 128), f32)
             field_b[(a + 1) * 10 + side] = jnp.zeros((NV, 128), f32)
 
+    for p in (4, 5):
+        for ref in (basis_hi, basis_lo):
+            ref[ELEMS + p, 0 : 6 * NV, :] = jnp.zeros((6 * NV, 128), bf16)
     for a in range(A_ROWS):
         for e in range(E_ROWS):
             el = a * E_ROWS + e
@@ -272,7 +277,48 @@
 
         return copies
 
-    def operator(field, field_out, slot_in, slot_out, shift, parity, copies):
+    def receive(copies, parity, slot):
+        def keep(p):
+            if slot < 6:
+                fh, fl = split(halo_in[parity, p])
+                basis_hi[ELEMS + p, slot * NV : (slot + 1) * NV, :] = fh
+                basis_lo[ELEMS + p, slot * NV : (slot + 1) * NV, :] = fl
+
+        copies[0].wait()
+        copies[1].wait()
+        for p in range(4):
+            keep(p)
+
+        @pl.when(has_above)
+        def _():
+            copies[2].wait_send()
+            copies[3].wait_recv()
+            keep(5)
+
+        @pl.when(has_below)
+        def _():
+            copies[3].wait_send()
+            copies[2].wait_recv()
+            keep(4)
+
+    def unpack(field, faces):
+        for p in range(2):
+            for k in range(4):
+                e = 4 * p + k
+                field[e + 1] = pltpu.roll(faces[p], (48 - 16 * k) % 128, 1)
+                field[5 * 10 + e + 1] = pltpu.roll(faces[2 + p], (128 - 16 * k) % 128, 1)
+
+        @pl.when(has_below)
+        def _():
+            for k in range(A_ROWS):
+                field[(k + 1) * 10] = pltpu.roll(faces[4], 3 - k, 1)
+
+        @pl.when(has_above)
+        def _():
+            for k in range(A_ROWS):
+                field[(k + 1) * 10 + E_ROWS + 1] = pltpu.roll(faces[5], (128 - k) % 128, 1)
+
+    def operator(field, field_out, slot_in, slot_out, shift, parity=0, copies=None, fill=lambda: None):
         @pl.loop(0, ELEMS // OWN)
         def _(group):
             for k in range(OWN):
@@ -287,36 +333,12 @@
                     here = here - shift
                 own[el] = y + x * here + (z + pltpu.roll(z, 64, 1))
 
-        copies[0].wait()
-        copies[1].wait()
-
-        @pl.when(has_above)
-        def _():
-            copies[2].wait_send()
-            copies[3].wait_recv()
-
-        @pl.when(has_below)
-        def _():
-            copies[3].wait_send()
-            copies[2].wait_recv()
-
-        for p in range(2):
-            for k in range(4):
-                e = 4 * p + k
-                field[e + 1] = pltpu.roll(halo_in[parity, p], (48 - 16 * k) % 128, 1)
-                field[5 * 10 + e + 1] = pltpu.roll(halo_in[parity, 2 + p], (128 - 16 * k) % 128, 1)
-
-        @pl.when(has_below)
-        def _():
-            for k in range(A_ROWS):
-                field[(k + 1) * 10] = pltpu.roll(halo_in[parity, 4], 3 - k, 1)
-
-        @pl.when(has_above)
-        def _():
-            for k in range(A_ROWS):
-                field[(k + 1) * 10 + E_ROWS + 1] = pltpu.roll(
-                    halo_in[parity, 5], (128 - k) % 128, 1
-                )
+        if copies is None:
+            unpack(field, halo_mix)
+        else:
+            fill()
+            receive(copies, parity, slot_in)
+            unpack(field, halo_in.at[parity])
 
         @pl.loop(0, ELEMS // PAIR)
         def _(bunch):
@@ -347,28 +369,31 @@
                     if field_out is not None:
                         field_out[padded(el)] = w
 
-    def gram(step):
-        first = KNOWN[step] * NV
-        stop = first + RAW
-
-        def body(quad, acc):
-            def four(ref, begin, end):
-                return jnp.concatenate([ref[quad * 4 + k, begin:end, :] for k in range(4)], axis=1)
-
-            wh, wl = four(basis_hi, first, stop), four(basis_lo, first, stop)
-            bh, bl = four(basis_hi, 0, stop), four(basis_lo, 0, stop)
+    def gram(step, begin, end):
+        known = KNOWN[step] * NV
+        first, stop = known + begin * NV, known + end * NV
+        rows = slice(begin * NV, end * NV)
+
+        def body(octet, acc):
+            def wide(ref, lower, upper):
+                return jnp.concatenate([ref[octet * 8 + k, lower:upper, :] for k in range(8)], axis=1)
+
+            wh, wl = wide(basis_hi, first, stop), wide(basis_lo, first, stop)
+            bh, bl = wide(basis_hi, 0, stop), wide(basis_lo, 0, stop)
             return acc + dot4(wh, wl, bh, bl, NT)
 
-        value = lax.fori_loop(0, ELEMS // 4, body, jnp.zeros((RAW, stop), f32))
+        value = lax.fori_loop(0, ELEMS // 8, body, jnp.zeros((stop - first, stop), f32))
         for i in range(step + 1):
-            piece = value[:, i * 128 : min(i * 128 + 128, stop)]
-            spare = 128 - piece.shape[1]
-            if spare:
-                piece = jnp.concatenate([piece, jnp.zeros((RAW, spare), f32)], axis=1)
-            sums[step][i * RAW : (i + 1) * RAW, :] = piece
-        used = (step + 1) * RAW
-        if SUM_ROWS[step] > used:
-            sums[step][used:, :] = jnp.zeros((SUM_ROWS[step] - used, 128), f32)
+            filled = max(0, min(128, stop - i * 128))
+            parts = [value[:, i * 128 : i * 128 + filled]] if filled else []
+            if filled < 128:
+                parts.append(jnp.zeros((stop - first, 128 - filled), f32))
+            piece = jnp.concatenate(parts, axis=1) if len(parts) > 1 else parts[0]
+            sums[step][i * RAW + begin * NV : i * RAW + end * NV, :] = piece
+
+    def settle(table):
+        upper = (iota((RAW, RAW), 0) < 2 * NV) & (iota((RAW, RAW), 1) >= 2 * NV)
+        return jnp.where(upper, table.T, table)
 
     def all_sum(step, work):
         size = SUM_ROWS[step] // n_dep
@@ -436,26 +461,33 @@
             [total[step][i * RAW : (i + 1) * RAW, :] for i in range(step + 1)], axis=1
         )
 
-    def mix(step, table):
-        first = KNOWN[step] * NV
-        stop = first + RAW
+    def mix(table, first, stop, reach, to_field=True):
         th, tl = split(table)
+
+        def two(el, ghost):
+            def both(ref):
+                return jnp.concatenate(
+                    [ref[el, 0 : reach * NV, :], ref[el + 1, 0 : reach * NV, :]], axis=1
+                )
+
+            fresh = dot3(th, tl, both(basis_hi), both(basis_lo))
+            fh, fl = split(fresh)
+            for half in range(2):
+                cut = slice(half * 128, half * 128 + 128)
+                basis_hi[el + half, first * NV : stop * NV, :] = fh[:, cut]
+                basis_lo[el + half, first * NV : stop * NV, :] = fl[:, cut]
+                if to_field and ghost:
+                    halo_mix[el + half - ELEMS] = fresh[:, cut]
+                elif to_field:
+                    field_a[padded(el + half)] = fresh[:, cut]
 
         @pl.loop(0, ELEMS // MIX)
         def _(bunch):
             for k in range(0, MIX, 2):
-                el = bunch * MIX + k
-
-                def both(ref):
-                    return jnp.concatenate([ref[el, 0:stop, :], ref[el + 1, 0:stop, :]], axis=1)
-
-                fresh = dot3(th, tl, both(basis_hi), both(basis_lo))
-                fh, fl = split(fresh)
-                for half in range(2):
-                    cut = slice(half * 128, half * 128 + 128)
-                    basis_hi[el + half, first:stop, :] = fh[:, cut]
-                    basis_lo[el + half, first:stop, :] = fl[:, cut]
-                    field_a[padded(el + half)] = fresh[-NV:, cut]
+                two(bunch * MIX + k, False)
+
+        for p in range(0, FACES, 2):
+            two(ELEMS + p, True)
 
     def extend(step, metric=None):
         begin, end = CUTS[step], CUTS[step + 1]
@@ -508,6 +540,11 @@
         if stage == 0:
             hess[...] = jnp.zeros_like(hess)
 
+    for step in range(STEPS):
+        used = (step + 1) * RAW
+        if SUM_ROWS[step] > used:
+            sums[step][used:, :] = jnp.zeros((SUM_ROWS[step] - used, 128), f32)
+
     pl.semaphore_wait(barrier, n_lat + n_dep - 2)
     copies = send_faces(field_a, 0)
 
@@ -551,46 +588,35 @@
 
     operator(field_a, field_b, 0, 1, None, 0, copies)
     copies = send_faces(field_b, 1)
-    operator(field_b, None, 1, 2, None, 1, copies)
-    gram(0)
-    table = all_sum(0, idle)[:, 0:RAW]
+    operator(field_b, field_a, 1, 2, None, 1, copies, lambda: gram(0, 0, 2))
+    copies = send_faces(field_a, 0)
+    gram(0, 2, 3)
+    table = settle(all_sum(0, idle)[:, 0:RAW])
     upper, inverse = eliminate(table)
-    mix(0, inverse)
-    copies = send_faces(field_a, 0)
-    lower = upper.T
-    start[...] = lower[0:NV, 0:NV]
-    column0 = dot_exact(inverse[0:NV, 0:NV], lower[NV : 2 * NV, :])
-    column1 = dot_exact(
-        inverse[NV : 2 * NV, NV : 2 * NV],
-        lower[2 * NV :, :] - dot_exact(lower[NV : 2 * NV, 0:NV], column0),
-    )
-    hess[0:NV, 0:RAW] = column0
-    hess[NV : 2 * NV, 0:RAW] = column1
-    on_diag = iota((NV, RAW), 0) == iota((NV, RAW), 1)
+    receive(copies, 0, 2)
+    mix(inverse[2 * NV :], 2, 3, 3)
     shift = jnp.sum(
-        jnp.sum(jnp.where(on_diag, column0, 0.0), axis=1, keepdims=True), axis=0, keepdims=True
+        jnp.sum(inverse[0:NV, 0:NV] * upper[0:NV, NV : 2 * NV], axis=1, keepdims=True),
+        axis=0,
+        keepdims=True,
     ) * (1.0 / NV)
 
-    for step in (1, 2):
+    def record_first():
+        lower = upper.T
+        start[...] = lower[0:NV, 0:NV]
+        column0 = dot_exact(inverse[0:NV, 0:NV], lower[NV : 2 * NV, :])
+        column1 = dot_exact(
+            inverse[NV : 2 * NV, NV : 2 * NV],
+            lower[2 * NV :, :] - dot_exact(lower[NV : 2 * NV, 0:NV], column0),
+        )
+        hess[0:NV, 0:RAW] = column0
+        hess[NV : 2 * NV, 0:RAW] = column1
+        mix(inverse[0 : 2 * NV, 0 : 2 * NV], 0, 2, 2, False)
+
+    def record(step, prods, tail, inverse):
         known = KNOWN[step]
         base = known * NV
         width = base + RAW
-        operator(field_a, field_b, known - 1, known, shift, 0, copies)
-        copies = send_faces(field_b, 1)
-        operator(field_b, field_a, known, known + 1, shift, 1, copies)
-        copies = send_faces(field_a, 0)
-        operator(field_a, None, known + 1, known + 2, shift, 0, copies)
-        gram(step)
-        table = all_sum(step, extend(step - 1))
-        prods = table[:, 0:base]
-        corner = table[:, base:width] - dot_exact(prods, prods, NT)
-        if step == 1:
-            upper, inverse = eliminate(corner)
-            mix(step, jnp.concatenate([-dot_exact(inverse, prods), inverse], axis=1))
-            copies = send_faces(field_a, 0)
-            tail = upper.T
-        else:
-            tail = eye(RAW)
         coefs = jnp.concatenate([prods, tail], axis=1)
         place = iota((NV, width), 1) - iota((NV, width), 0)
         row = CUTS[step]
@@ -599,11 +625,43 @@
             at = slice(k * NV, (k + 1) * NV)
             before = slice((k - 1) * NV, k * NV)
             column = coefs[at] + shift * coefs[before]
-            reach = base if step == 2 else base + (k - 1) * NV
+            reach = base if inverse is None else base + (k - 1) * NV
             column = column - dot_exact(coefs[before, 0:reach], hess[0:reach, 0:width])
-            if step == 1:
+            if inverse is not None:
                 column = dot_exact(inverse[before, before], column)
             hess[row + k * NV : row + (k + 1) * NV, 0:width] = column
+
+    def images(step, parity, field_last, fill):
+        known = KNOWN[step]
+        operator(field_a, field_b, known - 1, known, shift)
+        copies = send_faces(field_b, parity)
+        operator(field_b, field_a, known, known + 1, shift, parity, copies, fill)
+        copies = send_faces(field_a, 1 - parity)
+        operator(
+            field_a, field_last, known + 1, known + 2, shift, 1 - parity, copies, lambda: gram(step, 0, 2)
+        )
+
+    images(1, 1, field_b, record_first)
+    copies = send_faces(field_b, 1)
+    gram(1, 2, 3)
+    table = all_sum(1, extend(0))
+    prods = table[:, 0 : 3 * NV]
+    corner = settle(table[:, 3 * NV : 6 * NV]) - dot_exact(prods, prods, NT)
+    upper, inverse = eliminate(corner)
+    receive(copies, 1, 5)
+    weights = jnp.concatenate([-dot_exact(inverse, prods), inverse], axis=1)
+    mix(weights[2 * NV :], 5, 6, 6)
+
+    def record_second():
+        record(1, prods, upper.T, inverse)
+        mix(weights[0 : 2 * NV, 0 : 5 * NV], 3, 5, 5, False)
+
+    images(2, 0, None, record_second)
+    gram(2, 2, 3)
+    table = all_sum(2, extend(1))
+    prods = table[:, 0 : 6 * NV]
+    corner = settle(table[:, 6 * NV : 9 * NV]) - dot_exact(prods, prods, NT)
+    record(2, prods, eye(RAW), None)
 
     spread = hess[CUTS[2] : CUTS[3], 6 * NV : 9 * NV]
     last = extend(2, dot_exact(dot_exact(spread, corner), spread, NT))
@@ -647,8 +705,8 @@
             in_specs=[vmem] * 6,
             out_specs=vmem,
             scratch_shapes=[
-                V((ELEMS, 9 * NV, 128), bf16),
-                V((ELEMS, 9 * NV, 128), bf16),
+                V((ELEMS + FACES, 9 * NV, 128), bf16),
+                V((ELEMS + FACES, 9 * NV, 128), bf16),
                 V((ELEMS, 128, 128), bf16),
                 V((ELEMS, 128, 128), bf16),
                 V((60, NV, 128), f32),
@@ -661,8 +719,9 @@
                 V((ELEMS, 128), f32),
                 V((256, 128), bf16),
                 V((256, 128), bf16),
-                V((2, 6, NV, 128), f32),
-                V((2, 6, NV, 128), f32),
+                V((2, FACES, NV, 128), f32),
+                V((2, FACES, NV, 128), f32),
+                V((FACES, NV, 128), f32),
                 V((256, 384), f32),
                 V((NV, NV), f32),
                 {

time: 130 us -> 119 us (0.915)
  Pallas kernels: 128 us -> 117 us
    pallas_call x1, Pallas kernels: 128 us -> 117 us  [per_device(): pl.pallas_call(functools.partial(kernel, n_lat, n_dep), out_shape=jax.Sha...]
where the time goes in v3:
time: 119 us
  Pallas kernels  117 us (98%)
  local copies, waits for them, and re-layouts  1.87 us (2%)
    pallas_call x1, Pallas kernels, per_device(): pl.pallas_call(functools.partial(kernel, n_lat, n_dep), out_shape=jax.Sha...  117 us

profile of v3, /device:TPU:1, one launch (start us, length us, event | category | flops | bytes accessed | tf_op | source)
XLA Modules:
  0.0 118.8 jit_solution(5531398135080757946)
XLA Ops:
  0.0 116.9 %shard_map.64 = f32[4,8,32,128]{3,2,1,0:T(8,128)} custom-call(f32[4,8,128]{2,1,0:T(8,128)} %kappa_ref.1, f32[4,8,128]{2,1,0:T(8,128)} %state_ref.1, f32[4,8]{1,0:T(4,128)} %rate_ref.1, f32[3,64,64]{2,1,0:T(8,128)} %grads_ref.1, f32[4,32,128]{2,1,0:T(8,128)} %lift_ref.1, f32[4,8,32,128]{3,2,1,0:T(8,128)} %rhs_ref.1), custom_call_target="tpu_custom_call" | custom-call | tf_op jit(solution)/shard_map/pallas_call | solution.py:702
  116.9 1.9 %copy.8 = f32[4,8,32,128]{3,2,1,0:T(8,128)} copy(f32[4,8,32,128]{3,2,1,0:T(8,128)} %shard_map.64) | data formatting | bytes 1048576

commit v4 on v3

--- a/solution.py
+++ b/solution.py
@@ -46,6 +46,11 @@
     return both[:rows] + both[rows:] + dot(ah, bl, dims)
 
 
+def dot_wide(ah, al, both):
+    first = dot(ah, both)
+    return first[:, 0:128] + (first[:, 128:256] + dot(al, both[:, 0:128]))
+
+
 def dot4(ah, al, bh, bl, dims=NN):
     rows = ah.shape[0]
     stacked = jnp.concatenate([ah, al], axis=0)
@@ -75,26 +80,47 @@
         def column(x, k):
             return jnp.broadcast_to(x[:, k : k + 1], (8, width))
 
-        for k in range(begin, end, 2):
+        for k in range(begin, end, 4):
             p, q = k // 8, k % 8
             x = self.tiles[p]
-            head0, head1 = column(x, k), column(x, k + 1)
-            row0, row1 = x[q : q + 1, :], x[q + 1 : q + 2, :]
-            a, b, c = head0[q : q + 1], head1[q : q + 1], head1[q + 1 : q + 2]
+            head = [column(x, k + j) for j in range(4)]
+            row0, row1, row2, row3 = (x[q + j : q + j + 1, :] for j in range(4))
+            a, b, c = head[0][q : q + 1], head[1][q : q + 1], head[1][q + 1 : q + 2]
             a_inv = 1.0 / a
-            det_inv = 1.0 / (a * c - b * b)
             t = b * a_inv
+            d_inv = a * (1.0 / (a * c - b * b))
             scaled0 = row0 * a_inv
-            scaled1 = (row1 - t * row0) * (a * det_inv)
+            scaled1 = (row1 - t * row0) * d_inv
+            f02, f03 = head[2][q : q + 1] * a_inv, head[3][q : q + 1] * a_inv
+            f12 = (head[2][q + 1 : q + 2] - t * head[2][q : q + 1]) * d_inv
+            f13 = (head[3][q + 1 : q + 2] - t * head[3][q : q + 1]) * d_inv
+
+            def reduced(columns):
+                c0, c1, c2, c3 = columns
+                c1 = c1 - c0 * t
+                return c0, c1, c2 - c0 * f02 - c1 * f12, c3 - c0 * f03 - c1 * f13
+
+            h0, h1, h2, h3 = reduced(head)
+            row2 = row2 - h0[q + 2 : q + 3] * scaled0 - h1[q + 2 : q + 3] * scaled1
+            row3 = row3 - h0[q + 3 : q + 4] * scaled0 - h1[q + 3 : q + 4] * scaled1
+            a, b, c = h2[q + 2 : q + 3], h3[q + 2 : q + 3], h3[q + 3 : q + 4]
+            a_inv = 1.0 / a
+            t2 = b * a_inv
+            d_inv = a * (1.0 / (a * c - b * b))
+            scaled2 = row2 * a_inv
+            scaled3 = (row3 - t2 * row2) * d_inv
             for i in range(p, self.n // 8):
                 x = self.tiles[i]
-                c0 = head0 if i == p else column(x, k)
-                c1 = head1 if i == p else column(x, k + 1)
-                c1 = c1 - c0 * t
                 if i == p:
+                    c0, c1, c2, c3 = h0, h1, h2, h3 - h2 * t2
                     c0 = jnp.where(row > q, c0, 0.0)
                     c1 = jnp.where(row > q + 1, c1, 0.0)
-                self.tiles[i] = x - c0 * scaled0 - c1 * scaled1
+                    c2 = jnp.where(row > q + 2, c2, 0.0)
+                    c3 = jnp.where(row > q + 3, c3, 0.0)
+                else:
+                    c0, c1, c2, c3 = reduced([column(x, k + j) for j in range(4)])
+                    c3 = c3 - c2 * t2
+                self.tiles[i] = x - c0 * scaled0 - c1 * scaled1 - c2 * scaled2 - c3 * scaled3
 
     def finish(self):
         n, width = self.n, 2 * self.n
@@ -124,8 +150,7 @@
     out_ref,
     basis_hi,
     basis_lo,
-    stiff_hi,
-    stiff_lo,
+    stiff,
     field_a,
     field_b,
     own,
@@ -134,8 +159,7 @@
     kappa_z,
     diag,
     cross,
-    m_hi,
-    m_lo,
+    lift_both,
     halo_out,
     halo_in,
     halo_mix,
@@ -327,7 +351,7 @@
                 xl = basis_lo[el, slot_in * NV : (slot_in + 1) * NV, :]
                 x = field[padded(el)]
                 z = x * cross[pl.ds(el, 1), :]
-                y = dot3(xh, xl, stiff_hi[el], stiff_lo[el])
+                y = dot_wide(xh, xl, stiff[el])
                 here = diag[pl.ds(el, 1), :]
                 if shift is not None:
                     here = here - shift
@@ -359,7 +383,7 @@
                     )
                     vectors.append(jnp.concatenate([sideways, upright], axis=1))
                 ch, cl = split(jnp.concatenate(vectors, axis=0))
-                coupled = dot3(ch, cl, m_hi[...], m_lo[...])
+                coupled = dot_wide(ch, cl, lift_both[...])
                 for k in range(4):
                     el = bunch * PAIR + part_of * 4 + k
                     w = own[el] - coupled[k * NV : (k + 1) * NV]
@@ -524,7 +548,7 @@
             ysol[step][...] = dot_exact(inverse, state["right"])
 
         def run(stage):
-            first, second = size // 4 // 2 * 2, size * 3 // 4 // 2 * 2
+            first, second = size // 4 // 4 * 4, size * 3 // 4 // 4 * 4
             if stage == 0:
                 products()
                 state["work"].run(0, first)
@@ -563,8 +587,7 @@
         (place == 0).astype(f32), lift_ref[3]
     )
     mh, ml = split(jnp.concatenate(m_lat + [m_dep], axis=0))
-    m_hi[...] = mh
-    m_lo[...] = ml
+    lift_both[...] = jnp.concatenate([mh, ml], axis=1)
 
     @pl.loop(0, A_ROWS)
     def _(a):
@@ -583,8 +606,7 @@
                 block = jnp.where(same, blocks[k * 128 : (k + 1) * 128], 0.0)
                 bh, bl = split(block)
                 el = a * E_ROWS + two * 4 + k
-                stiff_hi[el] = bh
-                stiff_lo[el] = bl
+                stiff[el] = jnp.concatenate([bh, bl], axis=1)
 
     operator(field_a, field_b, 0, 1, None, 0, copies)
     copies = send_faces(field_b, 1)
@@ -707,8 +729,7 @@
             scratch_shapes=[
                 V((ELEMS + FACES, 9 * NV, 128), bf16),
                 V((ELEMS + FACES, 9 * NV, 128), bf16),
-                V((ELEMS, 128, 128), bf16),
-                V((ELEMS, 128, 128), bf16),
+                V((ELEMS, 128, 256), bf16),
                 V((60, NV, 128), f32),
                 V((60, NV, 128), f32),
                 V((ELEMS, NV, 128), f32),
@@ -717,8 +738,7 @@
                 V((ELEMS, 128), f32),
                 V((ELEMS, 128), f32),
                 V((ELEMS, 128), f32),
-                V((256, 128), bf16),
-                V((256, 128), bf16),
+                V((256, 256), bf16),
                 V((2, FACES, NV, 128), f32),
                 V((2, FACES, NV, 128), f32),
                 V((FACES, NV, 128), f32),
@@ -746,7 +766,7 @@
                 dma((STEPS, n_dep)),
             ],
             compiler_params=pltpu.CompilerParams(
-                collective_id=0, has_side_effects=True, vmem_limit_bytes=60 * 1024 * 1024
+                collective_id=0, has_side_effects=True, vmem_limit_bytes=24 * 1024 * 1024
             ),
         )(
             kappa, state, rate, grads, lift, rhs

time: 119 us -> 115 us (0.966)
  Pallas kernels: 117 us -> 109 us
  local copies, waits for them, and re-layouts: 1.87 us -> 5.68 us
    pallas_call x1, Pallas kernels: 117 us -> 109 us  [per_device(): pl.pallas_call(functools.partial(kernel, n_lat, n_dep), out_shape=jax.Sha...]
    unnamed x1 -> x13, local copies, waits for them, and re-layouts: 1.87 us -> 5.68 us
where the time goes in v4:
time: 115 us; the launch traced here: 114 us
  Pallas kernels  109 us (95%)
  local copies, waits for them, and re-layouts  5.68 us (5%)
    pallas_call x1, Pallas kernels, per_device(): pl.pallas_call(functools.partial(kernel, n_lat, n_dep), out_shape=jax.Sha...  109 us
    unnamed x13, local copies, waits for them, and re-layouts  5.68 us

profile of v4, /device:TPU:1, one launch (start us, length us, event | category | flops | bytes accessed | tf_op | source)
XLA Modules:
  0.0 114.3 jit_solution(17163172437015212420)
XLA Ops:
  0.0 0.0 copy-start
  0.0 1.0 copy-done
  1.0 0.0 copy-start.1
  1.0 0.9 copy-done.1
  1.9 0.0 copy-start.2
  1.9 0.8 copy-done.2
  2.8 0.0 copy-start.3
  2.8 0.7 copy-done.3
  3.5 0.0 copy-start.4
  3.5 0.7 copy-done.4
  4.2 0.0 copy-start.5
  4.2 0.7 copy-done.5
  4.9 108.6 %shard_map.64 = f32[4,8,32,128]{3,2,1,0:T(8,128)S(1)} custom-call(f32[4,8,128]{2,1,0:T(8,128)S(1)} %copy-done.3, f32[4,8,128]{2,1,0:T(8,128)S(1)} %copy-done.4, f32[4,8]{1,0:T(4,128)S(1)} %copy-done.5, f32[3,64,64]{2,1,0:T(8,128)S(1)} %copy-done.1, f32[4,32,128]{2,1,0:T(8,128)S(1)} %copy-done.2, f32[4,8,32,128]{3,2,1,0:T(8,128)S(1)} %copy-done), custom_call_target="tpu_custom_call" | custom-call | tf_op jit(solution)/shard_map/pallas_call | solution.py:724
  113.5 0.8 copy.8
Async XLA Ops:
  0.0 1.0 copy-start
  1.0 0.9 copy-start.1
  1.9 0.8 copy-start.2
  2.8 0.7 copy-start.3
  3.5 0.7 copy-start.4
  4.2 0.7 copy-start.5

commit v5 on v4

--- a/solution.py
+++ b/solution.py
@@ -141,13 +141,20 @@
 def kernel(
     n_lat,
     n_dep,
+    kappa_hbm,
+    state_hbm,
+    rate_hbm,
+    grads_hbm,
+    lift_hbm,
+    rhs_hbm,
+    out_ref,
     kappa_ref,
     state_ref,
     rate_ref,
     grads_ref,
     lift_ref,
     rhs_ref,
-    out_ref,
+    fetch_sem,
     basis_hi,
     basis_lo,
     stiff,
@@ -185,6 +192,20 @@
     lat = lax.axis_index("lat")
     dep = lax.axis_index("dep")
 
+    fetches = []
+    for index, (source, target) in enumerate(
+        (
+            (rhs_hbm, rhs_ref),
+            (kappa_hbm, kappa_ref),
+            (state_hbm, state_ref),
+            (rate_hbm, rate_ref),
+            (grads_hbm, grads_ref),
+            (lift_hbm, lift_ref),
+        )
+    ):
+        fetches.append(pltpu.make_async_copy(source, target, fetch_sem.at[index]))
+        fetches[-1].start()
+
     barrier = pltpu.get_barrier_semaphore()
     for k in range(1, n_dep):
         pl.semaphore_signal(
@@ -201,6 +222,9 @@
 
     def padded(el):
         return (el // E_ROWS + 1) * 10 + el % E_ROWS + 1
+
+    for fetch in fetches:
+        fetch.wait()
 
     touches = (node_x == 0) | (node_x == 3)
     touches = touches.astype(f32) + ((node_z == 0) | (node_z == 3)).astype(f32)
@@ -724,9 +748,16 @@
         out = pl.pallas_call(
             functools.partial(kernel, n_lat, n_dep),
             out_shape=jax.ShapeDtypeStruct((A_ROWS, E_ROWS, NV, 128), f32),
-            in_specs=[vmem] * 6,
+            in_specs=[pl.BlockSpec(memory_space=pltpu.HBM)] * 6,
             out_specs=vmem,
             scratch_shapes=[
+                V(kappa.shape, f32),
+                V(state.shape, f32),
+                V(rate.shape, f32),
+                V(grads.shape, f32),
+                V(lift.shape, f32),
+                V(rhs.shape, f32),
+                dma((6,)),
                 V((ELEMS + FACES, 9 * NV, 128), bf16),
                 V((ELEMS + FACES, 9 * NV, 128), bf16),
                 V((ELEMS, 128, 256), bf16),
@@ -766,7 +797,7 @@
                 dma((STEPS, n_dep)),
             ],
             compiler_params=pltpu.CompilerParams(
-                collective_id=0, has_side_effects=True, vmem_limit_bytes=24 * 1024 * 1024
+                collective_id=0, has_side_effects=True, vmem_limit_bytes=60 * 1024 * 1024
             ),
         )(
             kappa, state, rate, grads, lift, rhs

time: 115 us -> 112 us (0.974)
  local copies, waits for them, and re-layouts: 5.68 us -> 1.87 us
    unnamed x13 -> x1, local copies, waits for them, and re-layouts: 5.68 us -> 1.87 us
where the time goes in v5:
time: 112 us; the launch traced here: 111 us
  Pallas kernels  110 us (98%)
  local copies, waits for them, and re-layouts  1.87 us (2%)
    pallas_call x1, Pallas kernels, per_device(): pl.pallas_call(functools.partial(kernel, n_lat, n_dep), out_shape=jax.Sha...  110 us

profile of v5, /device:TPU:1, one launch (start us, length us, event | category | flops | bytes accessed | tf_op | source)
XLA Modules:
  0.0 111.4 jit_solution(11379541216584460856)
XLA Ops:
  0.0 109.5 %shard_map.64 = f32[4,8,32,128]{3,2,1,0:T(8,128)} custom-call(f32[4,8,128]{2,1,0:T(8,128)} %kappa_hbm.1, f32[4,8,128]{2,1,0:T(8,128)} %state_hbm.1, f32[4,8]{1,0:T(4,128)} %rate_hbm.1, f32[3,64,64]{2,1,0:T(8,128)} %grads_hbm.1, f32[4,32,128]{2,1,0:T(8,128)} %lift_hbm.1, f32[4,8,32,128]{3,2,1,0:T(8,128)} %rhs_hbm.1), custom_call_target="tpu_custom_call" | custom-call | tf_op jit(solution)/shard_map/pallas_call | solution.py:748
  109.6 1.9 %copy.8 = f32[4,8,32,128]{3,2,1,0:T(8,128)} copy(f32[4,8,32,128]{3,2,1,0:T(8,128)} %shard_map.64) | data formatting | bytes 1048576
